TPU v7x, 32 devices: a whole 2x2x4 slice. The times are simulated.
32 devices in a mesh: term: 8 (over z, x), sector: 4 (over y, core).
Axes of the slice: x: 2, y: 2, z: 4, core: 2. Of those that a mesh axis runs over, the one named last changes fastest.
Arguments:
- psi_start: float32 [4, 384, 384], P('sector'), may hold values from -6 to 6
- diagonal: float32 [4, 384, 384], P('sector'), may hold values from -3 to 3
- left_ops: float32 [128, 384, 384], P(('term', 'sector')), may hold values from -0.3125 to 0.3125
- right_ops: float32 [128, 384, 384], P(('term', 'sector')), may hold values from -0.078125 to 0.078125
- pair_in: int32 [32, 4], P(('term', 'sector')), may hold values from 0 to 3
- pair_out: int32 [32, 4], P(('term', 'sector')), may hold values from 0 to 3
- pair_count: int32 [32], P(('term', 'sector')), may hold values from 1 to 4, as said below
Outputs:
- psi_final: float32 [4, 384, 384], P('sector')
- energies: float32 [2], replicated
Inputs may be any that keep to these rules, and one draw needn't show every extreme that they name: `pair_count`: some device has all 4 slots live in every draw.
All inputs are finite; a program needn't handle non-finite values.
Results may differ from a plain program's by a relative error of at most 0.00013.
Values sent between devices are 32-bit elements; how exact they have to be, the bound alone decides.
No kernel may reach another device: no remote copies, remote signals or barrier semaphores. Data moves between devices by JAX's collectives and lax.ppermute only.
A program may use at most 64 MiB of HBM per device.

v0:
```python
import jax
import jax.numpy as jnp
from jax import lax
from jax.sharding import PartitionSpec as P

ITERS = 2


epsilon = 1e-06


def apply_pairs(gathered, left_ops, right_ops, pair_in, pair_out, pair_count):

    def one_pair(pair_slot, partial_value):
        source = lax.dynamic_index_in_dim(gathered, pair_in[0, pair_slot], 0, keepdims=False)
        left_block = lax.dynamic_index_in_dim(left_ops, pair_slot, 0, keepdims=False)
        right_block = lax.dynamic_index_in_dim(right_ops, pair_slot, 0, keepdims=False)
        inner_prod = jnp.dot(left_block, source, precision=lax.Precision.HIGHEST)
        product = lax.dot_general(
            inner_prod, right_block, (((1,), (1,)), ((), ())), precision=lax.Precision.HIGHEST
        )
        target = pair_out[0, pair_slot]
        current = lax.dynamic_index_in_dim(partial_value, target, 0, keepdims=False)
        return lax.dynamic_update_index_in_dim(partial_value, current + product, target, 0)

    return lax.fori_loop(0, pair_count[0], one_pair, jnp.zeros(gathered.shape, jnp.float32))


def global_sums(values):
    return lax.psum((values[0],), "sector")


def sigma_blocks(vector, left_ops, right_ops, pair_in, pair_out, pair_count):
    gathered = lax.all_gather(vector, "sector", axis=0, tiled=True)
    partial_value = apply_pairs(gathered, left_ops, right_ops, pair_in, pair_out, pair_count)
    owned_sum = lax.psum_scatter(partial_value, "sector", scatter_dimension=0, tiled=True)
    return lax.psum(owned_sum, "term")


def shards(psi_start, diagonal, left_ops, right_ops, pair_in, pair_out, pair_count):
    vector = psi_start
    cell_total = float(
        psi_start.shape[0] * lax.axis_size("sector") * psi_start.shape[1] * psi_start.shape[2]
    )
    energies = []
    for sweep in range(ITERS):
        vec_share = vector
        squares = global_sums((jnp.sum(vec_share * vec_share),))[0]
        inverse_norm = 1.0 / jnp.sqrt(squares / cell_total + epsilon)
        normed = vector * inverse_norm
        sigma = sigma_blocks(normed, left_ops, right_ops, pair_in, pair_out, pair_count)
        product_sum = global_sums((jnp.sum(normed * sigma),))[0]
        rayleigh = product_sum / cell_total
        residual = sigma - rayleigh * normed
        correction = residual / jnp.maximum(jnp.abs(diagonal - rayleigh), 1.0)
        updated = normed - correction
        vector = updated
        energies.append(rayleigh)
    return (vector, jnp.stack(energies))


def solution(mesh):
    return jax.shard_map(
        shards,
        mesh=mesh,
        in_specs=(
            P("sector", None, None),
            P("sector", None, None),
            P(("term", "sector"), None, None),
            P(("term", "sector"), None, None),
            P(("term", "sector"), None),
            P(("term", "sector"), None),
            P(("term", "sector")),
        ),
        out_specs=(P("sector", None, None), P()),
        check_vma=False,
    )
```

profile of v0, /device:TPU:0, one launch (start us, length us, event | category | flops | bytes accessed | tf_op | source)
XLA Modules:
  0.0 407.0 jit_solution(11676332899711747829)
XLA Ops:
  9.1 9.0 %psum.42 = f32[]{:T(128)} all-reduce(f32[]{:T(128)} %multiply_reduce_fusion.3), channel_id=1, replica_groups=mesh['term'=8,'sector'=4] {'sector'}, use_global_device_ids=true, to_apply=%region_1.0 | all-reduce | flops 1 | bytes 8 | tf_op jit(solution)/shard_map/psum | solution.py:30
  20.7 24.4 %all-gather.3.cloned.1.call-done = f32[4,384,384]{2,1,0:T(8,128)} async-done(((f32[1,384,384]{2,1,0:T(8,128)}), f32[4,384,384]{2,1,0:T(8,128)}) %all-gather.3.cloned.1.call-update) | async-done | bytes 2359312 | tf_op jit(solution)/shard_map/all_gather | solution.py:34
  45.4 39.8 %while.20 = (s32[]{:T(128)}, f32[4,384,384]{2,1,0:T(8,128)S(1)}, s32[]{:T(128)}, s32[1,4]{1,0:T(1,128)S(1)}, f32[4,384,384]{2,1,0:T(8,128)}, /*index=5*/s32[1,4]...) while((s32[]{:T(128)}, f32[4,384,384]{2,1,0:T(8,128)S(1)}, ...), condition=%wide.region_3.4_spmd, body=%wide.region_2.3_spmd.sunk | while | flops 1359101952 | bytes 5308675 | solution.py:26
  50.2 2.5 fusion.40
  52.8 2.3 fusion.41
  60.0 2.5 fusion.40
  69.8 2.5 fusion.40
  79.6 2.5 fusion.40
  82.1 2.3 fusion.41
  86.6 32.8 %reduce-scatter.3.cloned.1.call-done = f32[1,384,384]{2,1,0:T(8,128)} async-done(((f32[4,384,384]{2,1,0:T(8,128)}), f32[1,384,384]{2,1,0:T(8,128)}) %reduce-scatter.3.cloned.1.call-update) | async-done | bytes 589840 | tf_op jit(solution)/shard_map/reduce_scatter | solution.py:36
  119.5 76.6 %all-reduce.3.cloned.1.call-done = f32[1,384,384]{2,1,0:T(8,128)} async-done(((f32[1,384,384]{2,1,0:T(8,128)}), f32[1,384,384]{2,1,0:T(8,128)}) %all-reduce.3.cloned.1.call-update) | async-done | bytes 589840 | tf_op jit(solution)/shard_map/psum | solution.py:37
  197.9 6.3 %psum.44 = f32[]{:T(128)} all-reduce(f32[]{:T(128)} %multiply_reduce_fusion.2), channel_id=1, replica_groups=mesh['term'=8,'sector'=4] {'sector'}, use_global_device_ids=true, to_apply=%region_7.8 | all-reduce | flops 1 | bytes 8 | tf_op jit(solution)/shard_map/psum | solution.py:30
  206.7 7.2 %psum.45 = f32[]{:T(128)} all-reduce(f32[]{:T(128)} %get-tuple-element.122), channel_id=1, replica_groups=mesh['term'=8,'sector'=4] {'sector'}, use_global_device_ids=true, to_apply=%region_9.10 | all-reduce | flops 1 | bytes 8 | tf_op jit(solution)/shard_map/psum | solution.py:30
  215.6 22.5 %all-gather.5.cloned.1.call-done = f32[4,384,384]{2,1,0:T(8,128)} async-done(((f32[1,384,384]{2,1,0:T(8,128)}), f32[4,384,384]{2,1,0:T(8,128)}) %all-gather.5.cloned.1.call-update) | async-done | bytes 2359312 | tf_op jit(solution)/shard_map/all_gather | solution.py:34
  238.2 39.8 %while.21 = (s32[]{:T(128)}, f32[4,384,384]{2,1,0:T(8,128)S(1)}, s32[]{:T(128)}, s32[1,4]{1,0:T(1,128)S(1)}, f32[4,384,384]{2,1,0:T(8,128)}, /*index=5*/s32[1,4]...) while((s32[]{:T(128)}, f32[4,384,384]{2,1,0:T(8,128)S(1)}, ...), condition=%wide.region_11.12_spmd, body=%wide.region_10.11_spmd.sunk | while | flops 1359101952 | bytes 5308675 | solution.py:26
  243.1 2.5 fusion.46
  245.7 2.3 fusion.47
  252.9 2.5 fusion.46
  262.7 2.5 fusion.46
  272.4 2.5 fusion.46
  275.0 2.3 fusion.47
  279.5 32.8 %reduce-scatter.5.cloned.1.call-done = f32[1,384,384]{2,1,0:T(8,128)} async-done(((f32[4,384,384]{2,1,0:T(8,128)}), f32[1,384,384]{2,1,0:T(8,128)}) %reduce-scatter.5.cloned.1.call-update) | async-done | bytes 589840 | tf_op jit(solution)/shard_map/reduce_scatter | solution.py:36
  312.3 76.5 %all-reduce.5.cloned.1.call-done = f32[1,384,384]{2,1,0:T(8,128)} async-done(((f32[1,384,384]{2,1,0:T(8,128)}), f32[1,384,384]{2,1,0:T(8,128)}) %all-reduce.5.cloned.1.call-update) | async-done | bytes 589840 | tf_op jit(solution)/shard_map/psum | solution.py:37
  390.6 6.3 %psum.47 = f32[]{:T(128)} all-reduce(f32[]{:T(128)} %multiply_reduce_fusion), channel_id=1, replica_groups=mesh['term'=8,'sector'=4] {'sector'}, use_global_device_ids=true, to_apply=%region_15.16 | all-reduce | flops 1 | bytes 8 | tf_op jit(solution)/shard_map/psum | solution.py:30
  (54 shorter events, 30.6 us)
Async XLA Ops:
  7.2 38.2 %copy-start.4 = (s32[1,4]{1,0:T(1,128)S(1)}, s32[1,4]{1,0:T(1,128)}, u32[]{:S(2)}) copy-start(s32[1,4]{1,0:T(1,128)} %param.16) | copy-start | bytes 52
  7.2 38.2 %copy-start.5 = (s32[1,4]{1,0:T(1,128)S(1)}, s32[1,4]{1,0:T(1,128)}, u32[]{:S(2)}) copy-start(s32[1,4]{1,0:T(1,128)} %param.15) | copy-start | bytes 52
  7.2 38.0 %all-gather.3.cloned.1.call-start = ((), (), s32[]{:S(2)}) async-start(), calls=%async_computation.2 | async-start | bytes 2949120 | tf_op jit(solution)/shard_map/all_gather | solution.py:34
  20.7 98.7 %reduce-scatter.3.cloned.1.call-start = ((), (), s32[]{:S(2)}) async-start(), calls=%async_computation.3 | async-start | bytes 2949120 | tf_op jit(solution)/shard_map/reduce_scatter | solution.py:36
  85.1 1.4 copy-start.1
  85.1 111.0 %copy-start.2 = (f32[1,384,384]{2,1,0:T(8,128)S(1)}, f32[1,384,384]{2,1,0:T(8,128)}, u32[]{:S(2)}) copy-start(f32[1,384,384]{2,1,0:T(8,128)} %param.11) | copy-start | bytes 1769476
  85.2 119.7 %copy-start.3 = (f32[1,384,384]{2,1,0:T(8,128)S(1)}, f32[1,384,384]{2,1,0:T(8,128)}, u32[]{:S(2)}) copy-start(f32[1,384,384]{2,1,0:T(8,128)} %param.12) | copy-start | bytes 1769476
  86.6 109.5 %all-reduce.3.cloned.1.call-start = ((), (), s32[]{:S(2)}) async-start(), calls=%async_computation.4 | async-start | bytes 1179648 | tf_op jit(solution)/shard_map/psum | solution.py:37
  119.5 118.6 %all-gather.5.cloned.1.call-start = ((), (), s32[]{:S(2)}) async-start(), calls=%async_computation.5 | async-start | bytes 2949120 | tf_op jit(solution)/shard_map/all_gather | solution.py:34
  215.5 96.8 %reduce-scatter.5.cloned.1.call-start = ((), (), s32[]{:S(2)}) async-start(), calls=%async_computation.6 | async-start | bytes 2949120 | tf_op jit(solution)/shard_map/reduce_scatter | solution.py:36
  278.0 1.4 copy-start
  279.4 109.4 %all-reduce.5.cloned.1.call-start = ((), (), s32[]{:S(2)}) async-start(), calls=%async_computation.7 | async-start | bytes 1179648 | tf_op jit(solution)/shard_map/psum | solution.py:37
Sparse Core Ops, SparseCore 0:
  20.8 24.3 all-gather.2
  86.7 32.6 reduce-scatter.2
  122.8 73.2 all-reduce.2
  215.6 22.4 all-gather.4
  279.6 32.6 reduce-scatter.4
  315.5 73.2 all-reduce.4
where the time goes:
time: 409 us; the launch traced here: 407 us
  waiting for transfers between devices  266 us (65%)
  matrix products  38.7 us (9%)
  loops' own time  35.8 us (9%)
  blocking collectives  28.7 us (7%)
  between operations  16.9 us (4%)
  other arithmetic  12.8 us (3%)
  local copies, waits for them, and re-layouts  8.2 us (2%)
    psum x2, waiting for transfers between devices, sigma_blocks(): return lax.psum(owned_sum, 'term')  153 us
    reduce_scatter x2, waiting for transfers between devices, sigma_blocks(): lax.psum_scatter(partial_value, 'sector', scatter_dimension=0, tiled=True)  65.6 us
    all_gather x2, waiting for transfers between devices, sigma_blocks(): gathered = lax.all_gather(vector, 'sector', axis=0, tiled=True)  47 us
    another operation x2, loops' own time, apply_pairs(): lax.fori_loop(0, pair_count[0], one_pair, jnp.zeros(gathered.shape, jnp.f...  35.8 us
    psum x4, blocking collectives, global_sums(): return lax.psum((values[0],), 'sector')  28.7 us
    dot_general x8, matrix products, one_pair(): inner_prod = jnp.dot(left_block, source, precision=lax.Precision.HIGHEST)  20 us
    dot_general x8, matrix products, one_pair(): lax.dot_general(inner_prod, right_block, (((1,), (1,)), ((), ())), precis...  18.6 us
  transfers between devices with their start and end apart: 6, of which 6 were waited for; matrix products, arithmetic and copies ran while one was open for 0% of the time, Pallas kernels for 0%

commit v1 on v0

v1 whole, which is shorter than its diff:
```python
import functools

import jax
import jax.numpy as jnp
from jax import lax
from jax.experimental import pallas as pl
from jax.experimental.pallas import tpu as pltpu
from jax.sharding import PartitionSpec as P

ITERS = 2
AXES = ("term", "sector")
LANE_ROWS = 8

epsilon = 1e-06

VMEM = pl.BlockSpec(memory_space=pltpu.VMEM)
SMEM = pl.BlockSpec(memory_space=pltpu.SMEM)
F32 = jnp.float32
BF16 = jnp.bfloat16

ORDERS = (
    (("sector", 1), ("term", 0), ("term", 1)),
    (("term", 1), ("sector", 1), ("term", 0)),
)


def bit_of(axis, bit):
    return (lax.axis_index(axis) >> bit) & 1


def order_bits(core):
    a = [bit_of(axis, bit) for axis, bit in ORDERS[0]]
    b = [bit_of(axis, bit) for axis, bit in ORDERS[1]]
    return [jnp.where(core == 0, x, y) for x, y in zip(a, b)]


def place(core, bits, quarter):
    b1, b2, b3 = bits
    sector = jnp.where(core == 0, 2 * b1, 2 * b2 + 1)
    row = jnp.where(core == 0, 2 * b2 + b3, 2 * b1 + b3) * quarter
    return sector, pl.multiple_of(row, 8)


def split(x):
    high = x.astype(BF16)
    return high, (x - high.astype(F32)).astype(BF16)


def prep_kernel(left_ref, right_ref, lh_ref, ll_ref, rh_ref, rl_ref):
    lh_ref[...], ll_ref[...] = split(left_ref[...])
    rh_ref[...], rl_ref[...] = split(right_ref[...])


def prepare(left_ops, right_ops):
    pairs, b, _ = left_ops.shape
    spec = pl.BlockSpec((1, b, b), lambda i: (i, 0, 0))
    return pl.pallas_call(
        prep_kernel,
        grid=(pairs,),
        in_specs=[spec] * 2,
        out_specs=[spec] * 4,
        out_shape=[jax.ShapeDtypeStruct(left_ops.shape, BF16)] * 4,
        cost_estimate=pl.CostEstimate(
            flops=4 * left_ops.size, bytes_accessed=16 * left_ops.size, transcendentals=0
        ),
    )(left_ops, right_ops)


def apply_kernel(first, cells, *refs):
    (in_ref, out_ref, count_ref, p0, p1, p2, p3, lh, ll, rh, rl,
     send_ref, keep_ref, inv_ref, vec, vh, vl, acc) = refs
    sectors, b, _ = vec.shape
    quarter = b // 4
    me = lax.axis_index("sector")
    core = me & 1
    total = jnp.zeros((1, b), F32)
    for number, piece in enumerate((p0, p1, p2, p3)):
        if first:
            chunks = [(me ^ number, (0), 0, b)]
        else:
            of = core if number < 2 else 1 - core
            base = order_bits(of)
            chunks = []
            for k in range(4):
                bits = (base[0] ^ (number & 1), base[1] ^ (k >> 1), base[2] ^ (k & 1))
                sector, row = place(of, bits, quarter)
                chunks.append((sector, row, k * quarter, quarter))
        for sector, row, start, rows in chunks:
            x = piece[start:start + rows, :]
            high, low = split(x)
            vec[sector, pl.ds(row, rows), :] = x
            vh[sector, pl.ds(row, rows), :] = high
            vl[sector, pl.ds(row, rows), :] = low
            total += jnp.sum(x * x, axis=0, keepdims=True)
    inv = lax.rsqrt(jnp.broadcast_to(jnp.sum(total, axis=1, keepdims=True), (LANE_ROWS, b)) / cells + epsilon)
    inv_ref[...] = inv
    acc[...] = jnp.zeros_like(acc)

    def one_pair(p, carry):
        source = in_ref[0, p]
        target = out_ref[0, p]
        dot = functools.partial(jnp.dot, preferred_element_type=F32)
        a_h, a_l = lh[p], ll[p]
        x_h, x_l = vh[source], vl[source]
        inner = dot(a_h, x_h) + (dot(a_h, x_l) + dot(a_l, x_h))
        i_h, i_l = split(inner)
        r_h, r_l = rh[p], rl[p]
        nt = functools.partial(
            lax.dot_general, dimension_numbers=(((1,), (1,)), ((), ())), preferred_element_type=F32
        )
        acc[target] += nt(i_h, r_h) + (nt(i_h, r_l) + nt(i_l, r_h))
        return carry

    lax.fori_loop(0, count_ref[0], one_pair, 0)
    scale = inv[:1, :]
    rho = jnp.zeros((1, b), F32)
    for dest, of in ((send_ref, 1 - core), (keep_ref, core)):
        for j in range(8):
            sector, row = place(of, (j >> 2, (j >> 1) & 1, j & 1), quarter)
            x = acc[sector, pl.ds(row, quarter), :] * scale
            dest[j * quarter:(j + 1) * quarter, :] = x
            rho += jnp.sum(x * vec[sector, pl.ds(row, quarter), :], axis=0, keepdims=True)
    rho = jnp.broadcast_to(jnp.sum(rho * scale, axis=1, keepdims=True), (LANE_ROWS, b)) / cells
    send_ref[8 * quarter:, :] = rho
    keep_ref[8 * quarter:, :] = rho


def apply_pairs(first, cells, sectors, index, pieces, ops):
    pairs, b, _ = ops[0].shape
    rows = sectors * b // 2 + LANE_ROWS
    half = jax.ShapeDtypeStruct((rows, b), F32)
    return pl.pallas_call(
        functools.partial(apply_kernel, first, cells),
        in_specs=[SMEM] * 3 + [VMEM] * 8,
        out_specs=[VMEM] * 3,
        out_shape=[half, half, jax.ShapeDtypeStruct((LANE_ROWS, b), F32)],
        scratch_shapes=[
            pltpu.VMEM((sectors, b, b), F32),
            pltpu.VMEM((sectors, b, b), BF16),
            pltpu.VMEM((sectors, b, b), BF16),
            pltpu.VMEM((sectors, b, b), F32),
        ],
        compiler_params=pltpu.CompilerParams(vmem_limit_bytes=32 << 20),
    )(*index, *pieces, *ops)


def combine_kernel(step, keep_ref, recv_ref, send_ref, next_ref):
    rows = send_ref.shape[0] - LANE_ROWS
    bit = order_bits(bit_of("sector", 0))[step]
    for dest, which in ((send_ref, 1 - bit), (next_ref, bit)):
        at = pl.ds(pl.multiple_of(which * rows, 8), rows)
        dest[:rows, :] = keep_ref[at, :] + recv_ref[at, :]
        dest[rows:, :] = keep_ref[2 * rows:, :] + recv_ref[2 * rows:, :]


def combine(step, keep, recv):
    rows = (keep.shape[0] - LANE_ROWS) // 2 + LANE_ROWS
    shape = jax.ShapeDtypeStruct((rows, keep.shape[1]), F32)
    return pl.pallas_call(
        functools.partial(combine_kernel, step),
        in_specs=[VMEM] * 2,
        out_specs=[VMEM] * 2,
        out_shape=[shape] * 2,
    )(keep, recv)


def update_kernel(mine_ref, recv_ref, vec_ref, inv_ref, diag_ref, new_ref, energy_ref):
    rows = new_ref.shape[0]
    rho = mine_ref[rows:, :] + recv_ref[rows:, :]
    energy_ref[...] = rho[:, :energy_ref.shape[1]]
    rho = rho[:1, :]
    normed = vec_ref[...] * inv_ref[:1, :]
    sigma = mine_ref[:rows, :] + recv_ref[:rows, :]
    residual = sigma - rho * normed
    new_ref[...] = normed - residual / jnp.maximum(jnp.abs(diag_ref[...] - rho), 1.0)


def update(mine, recv, vec, inv, diag):
    return pl.pallas_call(
        update_kernel,
        in_specs=[VMEM] * 5,
        out_specs=[VMEM] * 2,
        out_shape=[
            jax.ShapeDtypeStruct(vec.shape, F32),
            jax.ShapeDtypeStruct((LANE_ROWS, 128), F32),
        ],
    )(mine, recv, vec, inv, diag)


def flips(mesh_shape, dims):
    terms, sectors = mesh_shape
    pairs = []
    for t in range(terms):
        for s in range(sectors):
            axis, bit = dims[s & 1]
            u, v = (t ^ (1 << bit), s) if axis == "term" else (t, s ^ (1 << bit))
            pairs.append((t * sectors + s, u * sectors + v))
    return pairs


def shards(mesh_shape, psi_start, diagonal, left_ops, right_ops, pair_in, pair_out, pair_count):
    terms, sectors = mesh_shape
    b = psi_start.shape[1]
    quarter = b // 4
    cells = float(sectors * b * b)
    index = (pair_in, pair_out, pair_count)

    def swap(x, *dims):
        return lax.ppermute(x, AXES, flips(mesh_shape, dims * 2 if len(dims) == 1 else dims))

    steps = list(zip(*ORDERS))
    core_step = ("sector", 0)
    rest = [("term", bit) for bit in range(2, terms.bit_length() - 1)]
    core = bit_of("sector", 0)
    _, row = place(core, order_bits(core), quarter)

    own = psi_start[0]
    across = swap(own, ("sector", 1))
    beside = swap(own, core_step)
    ops = prepare(left_ops, right_ops)
    corner = swap(across, core_step)
    pieces = (own, beside, across, corner)
    vec = lax.dynamic_slice(own, (row, 0), (quarter, b))
    diag = lax.dynamic_slice(diagonal[0], (row, 0), (quarter, b))
    energies = []
    for sweep in range(ITERS):
        send, keep, inv = apply_pairs(sweep == 0, cells, sectors, index, pieces, ops)
        recv = swap(send, core_step)
        for number, step in enumerate(steps):
            send, keep = combine(number, keep, recv)
            recv = swap(send, *step)
        mine = keep + recv
        for step in rest[:-1]:
            mine = mine + swap(mine, step)
        recv = swap(mine, rest[-1])
        vec, energy = update(mine, recv, vec, inv, diag)
        energies.append(energy[0, 0])
        last = sweep == ITERS - 1
        if not last:
            part = jnp.concatenate([vec, swap(vec, *steps[2])], 0)
            part = jnp.concatenate([part, swap(part, *steps[1])], 0)
            far = swap(part, *steps[0])
            pieces = (part, far, swap(part, core_step), swap(far, core_step))
    other = swap(vec, *steps[2])
    bits = order_bits(core)
    half = jnp.where(bits[2] == 0, jnp.concatenate([vec, other], 0), jnp.concatenate([other, vec], 0))
    last_step = (ORDERS[0][1], ORDERS[1][0])
    other = swap(half, *last_step)
    bit = jnp.where(core == 0, bits[1], bits[0])
    block = jnp.where(bit == 0, jnp.concatenate([half, other], 0), jnp.concatenate([other, half], 0))
    return block[None], jnp.stack(energies)


def solution(mesh):
    mesh_shape = (mesh.shape["term"], mesh.shape["sector"])
    return jax.shard_map(
        functools.partial(shards, mesh_shape),
        mesh=mesh,
        in_specs=(
            P("sector", None, None),
            P("sector", None, None),
            P(("term", "sector"), None, None),
            P(("term", "sector"), None, None),
            P(("term", "sector"), None),
            P(("term", "sector"), None),
            P(("term", "sector")),
        ),
        out_specs=(P("sector", None, None), P()),
        check_vma=False,
    )
```

time: 409 us -> 184 us (0.45)
  waiting for transfers between devices: 266 us -> 88.3 us
  matrix products: 38.7 us -> 0 us
  loops' own time: 35.8 us -> 0 us
  Pallas kernels: 0 us -> 33 us
  starting transfers between devices: 0.24 us -> 31.8 us
  blocking collectives: 28.7 us -> 0 us
  between operations: 16.9 us -> 1.44 us
  local copies, waits for them, and re-layouts: 8.2 us -> 22.3 us
  other arithmetic: 12.8 us -> 6.58 us
    psum x2 -> x0, waiting for transfers between devices: 153 us -> none  [sigma_blocks(): return lax.psum(owned_sum, 'term')]
    ppermute x0 -> x20, waiting for transfers between devices: none -> 88.3 us  [swap(): lax.ppermute(x, AXES, flips(mesh_shape, dims * 2 if len(dims) == 1 else d...]
    reduce_scatter x2 -> x0, waiting for transfers between devices: 65.6 us -> none  [sigma_blocks(): lax.psum_scatter(partial_value, 'sector', scatter_dimension=0, tiled=True)]
    all_gather x2 -> x0, waiting for transfers between devices: 47 us -> none  [sigma_blocks(): gathered = lax.all_gather(vector, 'sector', axis=0, tiled=True)]
    dot_general x16 -> x0, matrix products: 38.7 us -> none  [the longest x8 20 us: one_pair(): inner_prod = jnp.dot(left_block, source, precision=lax.Precision.HIGHEST)]
    another operation x2 -> x0, loops' own time: 35.8 us -> none  [apply_pairs(): lax.fori_loop(0, pair_count[0], one_pair, jnp.zeros(gathered.shape, jnp.f...]
    pallas_call x0 -> x11, Pallas kernels: none -> 33 us  [the longest x6 13.6 us: combine(): pl.pallas_call(functools.partial(combine_kernel, step), in_specs=[VMEM] *...]
    ppermute x0 -> x20, starting transfers between devices: none -> 31.8 us  [swap(): lax.ppermute(x, AXES, flips(mesh_shape, dims * 2 if len(dims) == 1 else d...]
  transfers between devices with their start and end apart: 6 -> 20, of which waited for: 6 -> 17; matrix products, arithmetic and copies ran while one was open for 0% -> 4% of each run, Pallas kernels for 0% -> 3%
where the time goes in v1:
time: 184 us; the launch traced here: 183 us
  waiting for transfers between devices  88.3 us (48%)
  Pallas kernels  33 us (18%)
  starting transfers between devices  31.8 us (17%)
  local copies, waits for them, and re-layouts  22.3 us (12%)
  other arithmetic  6.58 us (4%)
    ppermute x20, waiting for transfers between devices, swap(): lax.ppermute(x, AXES, flips(mesh_shape, dims * 2 if len(dims) == 1 else d...  88.3 us
    ppermute x20, starting transfers between devices, swap(): lax.ppermute(x, AXES, flips(mesh_shape, dims * 2 if len(dims) == 1 else d...  31.8 us
    unnamed x54, local copies, waits for them, and re-layouts  18.5 us
    pallas_call x6, Pallas kernels, combine(): pl.pallas_call(functools.partial(combine_kernel, step), in_specs=[VMEM] *...  13.6 us
    pallas_call x2, Pallas kernels, apply_pairs(): pl.pallas_call(functools.partial(apply_kernel, first, cells), in_specs=[S...  10.5 us
    pallas_call x1, Pallas kernels, prepare(): pl.pallas_call(prep_kernel, grid=(pairs,), in_specs=[spec] * 2, out_specs...  5.05 us
    pallas_call x2, Pallas kernels, update(): pl.pallas_call(update_kernel, in_specs=[VMEM] * 5, out_specs=[VMEM] * 2,...  3.89 us
  transfers between devices with their start and end apart: 20, of which 17 were waited for; matrix products, arithmetic and copies ran while one was open for 4% of the time, Pallas kernels for 3%

profile of v1, /device:TPU:0, one launch (start us, length us, event | category | flops | bytes accessed | tf_op | source)
XLA Modules:
  0.0 183.4 jit_solution(1737241604787180394)
XLA Ops:
  0.6 3.1 %collective-permute-start.1 = (f32[384,384]{1,0:T(8,128)}, f32[384,384]{1,0:T(8,128)S(1)}, u32[]{:S(2)}, u32[]{:S(2)}) collective-permute-start(f32[384,384]{1,0:T(8,128)} %bitcast.9), channel_id=1, source_target_pairs={{0,2},{1,3},{2,0},{3,1},{4,6},{5,7},{6,4},{7,5},{8,10},{9,11},{10,... | collective-permute-start | bytes 1769480 | tf_op jit(solution)/shard_map/ppermute | solution.py:209
  3.7 13.5 %collective-permute-done.1.refs_5_ = f32[384,384]{1,0:T(8,128)S(1)} collective-permute-done((f32[384,384]{1,0:T(8,128)}, f32[384,384]{1,0:T(8,128)S(1)}, u32[]{:S(2)}, u32[]{:S(2)}) %collective-permute-start.1) | collective-permute-done | bytes 589856 | tf_op jit(solution)/shard_map/ppermute | solution.py:209
  17.9 5.1 %shard_map.86 = (bf16[4,384,384]{2,1,0:T(8,128)(2,1)}, bf16[4,384,384]{2,1,0:T(8,128)(2,1)}, bf16[4,384,384]{2,1,0:T(8,128)(2,1)}, bf16[4,384,384]{2,1,0:T(8,128)(2,1)}) custom-call(f32[4,384,384]{2,1,0:T(8,128)} %left_ref.1, f32[4,384,384]{2,1,0:T(8,128)} %right_ref.1), custom_call_target="tpu_custom_call" | custom-call | flops 2359296 | bytes 9437184 | tf_op jit(solution)/shard_map/pallas_call | solution.py:57
  28.1 5.3 %shard_map.87 = (f32[776,384]{1,0:T(8,128)S(1)}, f32[776,384]{1,0:T(8,128)S(1)}, f32[8,384]{1,0:T(8,128)S(1)}) custom-call(s32[1,4]{1,0:T(1,128)S(1)} %copy-done.14, s32[1,4]{1,0:T(1,128)S(1)} %copy-done.15, s32[1]{0:T(128)S(6)} %copy.11.refs_2_, f32[384,384]{1,0:T(8,128)S(1)} %bitcast.11, f32[384,384]{1,0:T(8,128)S(1)} %collective-permute-done.refs_4_, ...), custom_call_target="tpu_custom_call" | custom-call | tf_op jit(solution)/shard_map/pallas_call | solution.py:132
  37.2 2.5 %collective-permute-done.3.recv_ref = f32[776,384]{1,0:T(8,128)S(1)} collective-permute-done((f32[776,384]{1,0:T(8,128)S(1)}, f32[776,384]{1,0:T(8,128)S(1)}, u32[]{:S(2)}, u32[]{:S(2)}) %collective-permute-start.3) | collective-permute-done | bytes 1191968 | tf_op jit(solution)/shard_map/ppermute | solution.py:209
  40.7 2.9 %shard_map.88 = (f32[392,384]{1,0:T(8,128)}, f32[392,384]{1,0:T(8,128)}) custom-call(f32[776,384]{1,0:T(8,128)} %copy-done.10, f32[776,384]{1,0:T(8,128)} %copy-done.16), custom_call_target="tpu_custom_call" | custom-call | tf_op jit(solution)/shard_map/pallas_call | solution.py:159
  45.3 8.5 %collective-permute-done.4.recv_ref = f32[392,384]{1,0:T(8,128)S(1)} collective-permute-done((f32[392,384]{1,0:T(8,128)}, f32[392,384]{1,0:T(8,128)S(1)}, u32[]{:S(2)}, u32[]{:S(2)}) %collective-permute-start.4) | collective-permute-done | bytes 602144 | tf_op jit(solution)/shard_map/ppermute | solution.py:209
  56.8 3.3 %collective-permute-start.5 = (f32[200,384]{1,0:T(8,128)}, f32[200,384]{1,0:T(8,128)S(1)}, u32[]{:S(2)}, u32[]{:S(2)}) collective-permute-start(f32[200,384]{1,0:T(8,128)} %get-tuple-element.37), channel_id=1, source_target_pairs={{0,4},{1,3},{2,6},{3,1},{4,0},{5,7},{6,2},{7,5},{8,12},{9,11},{10,... | collective-permute-start | bytes 921608 | tf_op jit(solution)/shard_map/ppermute | solution.py:209
  60.1 5.0 %collective-permute-done.5.recv_ref = f32[200,384]{1,0:T(8,128)S(1)} collective-permute-done((f32[200,384]{1,0:T(8,128)}, f32[200,384]{1,0:T(8,128)S(1)}, u32[]{:S(2)}, u32[]{:S(2)}) %collective-permute-start.5) | collective-permute-done | bytes 307232 | tf_op jit(solution)/shard_map/ppermute | solution.py:209
  69.3 3.9 %collective-permute-done.6 = f32[104,384]{1,0:T(8,128)S(1)} collective-permute-done((f32[104,384]{1,0:T(8,128)}, f32[104,384]{1,0:T(8,128)S(1)}, u32[]{:S(2)}, u32[]{:S(2)}) %collective-permute-start.6) | collective-permute-done | bytes 159776 | tf_op jit(solution)/shard_map/ppermute | solution.py:209
  74.2 3.2 %collective-permute-start.7 = (f32[104,384]{1,0:T(8,128)S(1)}, f32[104,384]{1,0:T(8,128)S(1)}, u32[]{:S(2)}, u32[]{:S(2)}) collective-permute-start(f32[104,384]{1,0:T(8,128)S(1)} %add.16.mine_ref), channel_id=1, source_target_pairs={{0,16},{1,17},{2,18},{3,19},{4,20},{5,21},{6,22},{7,23},{8,24},{9,... | collective-permute-start | bytes 479240 | tf_op jit(solution)/shard_map/ppermute | solution.py:209
  78.7 3.9 %collective-permute-done.7.recv_ref = f32[104,384]{1,0:T(8,128)S(1)} collective-permute-done((f32[104,384]{1,0:T(8,128)S(1)}, f32[104,384]{1,0:T(8,128)S(1)}, u32[]{:S(2)}, u32[]{:S(2)}) %collective-permute-start.7) | collective-permute-done | bytes 159776 | tf_op jit(solution)/shard_map/ppermute | solution.py:209
  86.0 4.6 %collective-permute-done.8 = f32[96,384]{1,0:T(8,128)S(1)} collective-permute-done((f32[96,384]{1,0:T(8,128)}, f32[96,384]{1,0:T(8,128)S(1)}, u32[]{:S(2)}, u32[]{:S(2)}) %collective-permute-start.8) | collective-permute-done | bytes 147488 | tf_op jit(solution)/shard_map/ppermute | solution.py:209
  94.1 4.2 %collective-permute-done.9 = f32[192,384]{1,0:T(8,128)S(1)} collective-permute-done((f32[192,384]{1,0:T(8,128)S(1)}, f32[192,384]{1,0:T(8,128)S(1)}, u32[]{:S(2)}, u32[]{:S(2)}) %collective-permute-start.9) | collective-permute-done | bytes 294944 | tf_op jit(solution)/shard_map/ppermute | solution.py:209
  100.0 8.4 %collective-permute-done.10.refs_4_ = f32[384,384]{1,0:T(8,128)S(1)} collective-permute-done((f32[384,384]{1,0:T(8,128)S(1)}, f32[384,384]{1,0:T(8,128)S(1)}, u32[]{:S(2)}, u32[]{:S(2)}) %collective-permute-start.10) | collective-permute-done | bytes 589856 | tf_op jit(solution)/shard_map/ppermute | solution.py:209
  112.9 5.1 %shard_map.92 = (f32[776,384]{1,0:T(8,128)S(1)}, f32[776,384]{1,0:T(8,128)S(1)}, f32[8,384]{1,0:T(8,128)S(1)}) custom-call(s32[1,4]{1,0:T(1,128)S(1)} %copy-done.14, s32[1,4]{1,0:T(1,128)S(1)} %copy-done.15, s32[1]{0:T(128)S(6)} %copy.11.refs_2_, f32[384,384]{1,0:T(8,128)S(1)} %constant_dynamic-update-slice_fusion.refs_3_, ...), custom_call_target="tpu_custom_call" | custom-call | tf_op jit(solution)/shard_map/pallas_call | solution.py:132
  124.9 2.8 %shard_map.93 = (f32[392,384]{1,0:T(8,128)}, f32[392,384]{1,0:T(8,128)}) custom-call(f32[776,384]{1,0:T(8,128)} %copy-done.9, f32[776,384]{1,0:T(8,128)} %copy-done.17), custom_call_target="tpu_custom_call" | custom-call | tf_op jit(solution)/shard_map/pallas_call | solution.py:159
  129.2 8.7 %collective-permute-done.14.recv_ref = f32[392,384]{1,0:T(8,128)S(1)} collective-permute-done((f32[392,384]{1,0:T(8,128)}, f32[392,384]{1,0:T(8,128)S(1)}, u32[]{:S(2)}, u32[]{:S(2)}) %collective-permute-start.14) | collective-permute-done | bytes 602144 | tf_op jit(solution)/shard_map/ppermute | solution.py:209
  140.9 3.2 %collective-permute-start.15 = (f32[200,384]{1,0:T(8,128)}, f32[200,384]{1,0:T(8,128)S(1)}, u32[]{:S(2)}, u32[]{:S(2)}) collective-permute-start(f32[200,384]{1,0:T(8,128)} %get-tuple-element.47), channel_id=1, source_target_pairs={{0,4},{1,3},{2,6},{3,1},{4,0},{5,7},{6,2},{7,5},{8,12},{9,11},{10,... | collective-permute-start | bytes 921608 | tf_op jit(solution)/shard_map/ppermute | solution.py:209
  144.1 5.0 %collective-permute-done.15.recv_ref = f32[200,384]{1,0:T(8,128)S(1)} collective-permute-done((f32[200,384]{1,0:T(8,128)}, f32[200,384]{1,0:T(8,128)S(1)}, u32[]{:S(2)}, u32[]{:S(2)}) %collective-permute-start.15) | collective-permute-done | bytes 307232 | tf_op jit(solution)/shard_map/ppermute | solution.py:209
  152.6 4.6 %collective-permute-done.16 = f32[104,384]{1,0:T(8,128)S(1)} collective-permute-done((f32[104,384]{1,0:T(8,128)}, f32[104,384]{1,0:T(8,128)S(1)}, u32[]{:S(2)}, u32[]{:S(2)}) %collective-permute-start.16) | collective-permute-done | bytes 159776 | tf_op jit(solution)/shard_map/ppermute | solution.py:209
  158.1 2.8 %collective-permute-start.17 = (f32[104,384]{1,0:T(8,128)S(1)}, f32[104,384]{1,0:T(8,128)S(1)}, u32[]{:S(2)}, u32[]{:S(2)}) collective-permute-start(f32[104,384]{1,0:T(8,128)S(1)} %add.20.mine_ref), channel_id=1, source_target_pairs={{0,16},{1,17},{2,18},{3,19},{4,20},{5,21},{6,22},{7,23},{8,24},{9,... | collective-permute-start | bytes 479240 | tf_op jit(solution)/shard_map/ppermute | solution.py:209
  161.0 5.4 %collective-permute-done.17.recv_ref = f32[104,384]{1,0:T(8,128)S(1)} collective-permute-done((f32[104,384]{1,0:T(8,128)S(1)}, f32[104,384]{1,0:T(8,128)S(1)}, u32[]{:S(2)}, u32[]{:S(2)}) %collective-permute-start.17) | collective-permute-done | bytes 159776 | tf_op jit(solution)/shard_map/ppermute | solution.py:209
  169.5 5.3 %collective-permute-done.18 = f32[96,384]{1,0:T(8,128)S(1)} collective-permute-done((f32[96,384]{1,0:T(8,128)}, f32[96,384]{1,0:T(8,128)S(1)}, u32[]{:S(2)}, u32[]{:S(2)}) %collective-permute-start.18) | collective-permute-done | bytes 147488 | tf_op jit(solution)/shard_map/ppermute | solution.py:209
  (92 shorter events, 61.8 us)
Async XLA Ops:
  0.6 77.4 %copy-start = (f32[1,384,384]{2,1,0:T(8,128)S(1)}, f32[1,384,384]{2,1,0:T(8,128)}, u32[]{:S(2)}) copy-start(f32[1,384,384]{2,1,0:T(8,128)} %param.8) | copy-start | bytes 1769476
  0.6 16.6 %collective-permute-start.1 = (f32[384,384]{1,0:T(8,128)}, f32[384,384]{1,0:T(8,128)S(1)}, u32[]{:S(2)}, u32[]{:S(2)}) collective-permute-start(f32[384,384]{1,0:T(8,128)} %bitcast.9), channel_id=1, source_target_pairs={{0,2},{1,3},{2,0},{3,1},{4,6},{5,7},{6,4},{7,5},{8,10},{9,11},{10,... | collective-permute-start | bytes 1769480 | tf_op jit(solution)/shard_map/ppermute | solution.py:209
  3.7 19.3 %collective-permute-start = (f32[384,384]{1,0:T(8,128)}, f32[384,384]{1,0:T(8,128)S(1)}, u32[]{:S(2)}, u32[]{:S(2)}) collective-permute-start(f32[384,384]{1,0:T(8,128)} %bitcast.10), channel_id=1, source_target_pairs={{0,1},{1,0},{2,3},{3,2},{4,5},{5,4},{6,7},{7,6},{8,9},{9,8},{10,11... | collective-permute-start | bytes 1769480 | tf_op jit(solution)/shard_map/ppermute | solution.py:209
  17.2 5.7 %collective-permute-start.2 = (f32[384,384]{1,0:T(8,128)S(1)}, f32[384,384]{1,0:T(8,128)S(1)}, u32[]{:S(2)}, u32[]{:S(2)}) collective-permute-start(f32[384,384]{1,0:T(8,128)S(1)} %collective-permute-done.1.refs_5_), channel_id=1, source_target_pairs={{0,1},{1,0},{2,3},{3,2},{4,5},{5,4},{6,7},{7,6},{8,9},{9,8},{10,11... | collective-permute-start | bytes 1769480 | tf_op jit(solution)/shard_map/ppermute | solution.py:209
  35.1 4.6 %collective-permute-start.3 = (f32[776,384]{1,0:T(8,128)S(1)}, f32[776,384]{1,0:T(8,128)S(1)}, u32[]{:S(2)}, u32[]{:S(2)}) collective-permute-start(f32[776,384]{1,0:T(8,128)S(1)} %get-tuple-element.33), channel_id=1, source_target_pairs={{0,1},{1,0},{2,3},{3,2},{4,5},{5,4},{6,7},{7,6},{8,9},{9,8},{10,11... | collective-permute-start | bytes 3575816 | tf_op jit(solution)/shard_map/ppermute | solution.py:209
  43.6 10.2 %collective-permute-start.4 = (f32[392,384]{1,0:T(8,128)}, f32[392,384]{1,0:T(8,128)S(1)}, u32[]{:S(2)}, u32[]{:S(2)}) collective-permute-start(f32[392,384]{1,0:T(8,128)} %get-tuple-element.35), channel_id=1, source_target_pairs={{0,2},{1,9},{2,0},{3,11},{4,6},{5,13},{6,4},{7,15},{8,10},{9,1},{1... | collective-permute-start | bytes 1806344 | tf_op jit(solution)/shard_map/ppermute | solution.py:209
  56.8 8.4 %collective-permute-start.5 = (f32[200,384]{1,0:T(8,128)}, f32[200,384]{1,0:T(8,128)S(1)}, u32[]{:S(2)}, u32[]{:S(2)}) collective-permute-start(f32[200,384]{1,0:T(8,128)} %get-tuple-element.37), channel_id=1, source_target_pairs={{0,4},{1,3},{2,6},{3,1},{4,0},{5,7},{6,2},{7,5},{8,12},{9,11},{10,... | collective-permute-start | bytes 921608 | tf_op jit(solution)/shard_map/ppermute | solution.py:209
  67.7 5.5 %collective-permute-start.6 = (f32[104,384]{1,0:T(8,128)}, f32[104,384]{1,0:T(8,128)S(1)}, u32[]{:S(2)}, u32[]{:S(2)}) collective-permute-start(f32[104,384]{1,0:T(8,128)} %get-tuple-element.39), channel_id=1, source_target_pairs={{0,8},{1,5},{2,10},{3,7},{4,12},{5,1},{6,14},{7,3},{8,0},{9,13},{1... | collective-permute-start | bytes 479240 | tf_op jit(solution)/shard_map/ppermute | solution.py:209
  74.1 8.4 %copy-start.18 = (f32[104,384]{1,0:T(8,128)}, f32[104,384]{1,0:T(8,128)S(1)}, u32[]{:S(2)}) copy-start(f32[104,384]{1,0:T(8,128)S(1)} %add.16.mine_ref) | copy-start | bytes 479236
  74.2 8.4 %collective-permute-start.7 = (f32[104,384]{1,0:T(8,128)S(1)}, f32[104,384]{1,0:T(8,128)S(1)}, u32[]{:S(2)}, u32[]{:S(2)}) collective-permute-start(f32[104,384]{1,0:T(8,128)S(1)} %add.16.mine_ref), channel_id=1, source_target_pairs={{0,16},{1,17},{2,18},{3,19},{4,20},{5,21},{6,22},{7,23},{8,24},{9,... | collective-permute-start | bytes 479240 | tf_op jit(solution)/shard_map/ppermute | solution.py:209
  83.2 27.1 %copy-start.2 = (bf16[4,384,384]{2,1,0:T(8,128)(2,1)S(1)}, bf16[4,384,384]{2,1,0:T(8,128)(2,1)}, u32[]{:S(2)}) copy-start(bf16[4,384,384]{2,1,0:T(8,128)(2,1)} %get-tuple-element.28.refs_7_) | copy-start | bytes 3538948
  83.2 27.1 %copy-start.4 = (bf16[4,384,384]{2,1,0:T(8,128)(2,1)S(1)}, bf16[4,384,384]{2,1,0:T(8,128)(2,1)}, u32[]{:S(2)}) copy-start(bf16[4,384,384]{2,1,0:T(8,128)(2,1)} %get-tuple-element.29.refs_8_) | copy-start | bytes 3538948
  85.3 5.4 %collective-permute-start.8 = (f32[96,384]{1,0:T(8,128)}, f32[96,384]{1,0:T(8,128)S(1)}, u32[]{:S(2)}, u32[]{:S(2)}) collective-permute-start(f32[96,384]{1,0:T(8,128)} %get-tuple-element.41.vec_ref), channel_id=1, source_target_pairs={{0,8},{1,5},{2,10},{3,7},{4,12},{5,1},{6,14},{7,3},{8,0},{9,13},{1... | collective-permute-start | bytes 442376 | tf_op jit(solution)/shard_map/ppermute | solution.py:209
  91.5 6.8 %collective-permute-start.9 = (f32[192,384]{1,0:T(8,128)S(1)}, f32[192,384]{1,0:T(8,128)S(1)}, u32[]{:S(2)}, u32[]{:S(2)}) collective-permute-start(f32[192,384]{1,0:T(8,128)S(1)} %pad_maximum_fusion), channel_id=1, source_target_pairs={{0,4},{1,3},{2,6},{3,1},{4,0},{5,7},{6,2},{7,5},{8,12},{9,11},{10,... | collective-permute-start | bytes 884744 | tf_op jit(solution)/shard_map/ppermute | solution.py:209
  98.4 9.9 %collective-permute-start.10 = (f32[384,384]{1,0:T(8,128)S(1)}, f32[384,384]{1,0:T(8,128)S(1)}, u32[]{:S(2)}, u32[]{:S(2)}) collective-permute-start(f32[384,384]{1,0:T(8,128)S(1)} %constant_dynamic-update-slice_fusion.refs_3_), channel_id=1, source_target_pairs={{0,2},{1,9},{2,0},{3,11},{4,6},{5,13},{6,4},{7,15},{8,10},{9,1},{1... | collective-permute-start | bytes 1769480 | tf_op jit(solution)/shard_map/ppermute | solution.py:209
  99.9 8.4 %collective-permute-start.11 = (f32[384,384]{1,0:T(8,128)S(1)}, f32[384,384]{1,0:T(8,128)S(1)}, u32[]{:S(2)}, u32[]{:S(2)}) collective-permute-start(f32[384,384]{1,0:T(8,128)S(1)} %constant_dynamic-update-slice_fusion.refs_3_), channel_id=1, source_target_pairs={{0,1},{1,0},{2,3},{3,2},{4,5},{5,4},{6,7},{7,6},{8,9},{9,8},{10,11... | collective-permute-start | bytes 1769480 | tf_op jit(solution)/shard_map/ppermute | solution.py:209
  108.3 2.0 %collective-permute-start.12 = (f32[384,384]{1,0:T(8,128)S(1)}, f32[384,384]{1,0:T(8,128)S(1)}, u32[]{:S(2)}, u32[]{:S(2)}) collective-permute-start(f32[384,384]{1,0:T(8,128)S(1)} %collective-permute-done.10.refs_4_), channel_id=1, source_target_pairs={{0,1},{1,0},{2,3},{3,2},{4,5},{5,4},{6,7},{7,6},{8,9},{9,8},{10,11... | collective-permute-start | bytes 1769480 | tf_op jit(solution)/shard_map/ppermute | solution.py:209
  119.7 4.2 %collective-permute-start.13 = (f32[776,384]{1,0:T(8,128)S(1)}, f32[776,384]{1,0:T(8,128)S(1)}, u32[]{:S(2)}, u32[]{:S(2)}) collective-permute-start(f32[776,384]{1,0:T(8,128)S(1)} %get-tuple-element.43), channel_id=1, source_target_pairs={{0,1},{1,0},{2,3},{3,2},{4,5},{5,4},{6,7},{7,6},{8,9},{9,8},{10,11... | collective-permute-start | bytes 3575816 | tf_op jit(solution)/shard_map/ppermute | solution.py:209
  127.7 10.2 %collective-permute-start.14 = (f32[392,384]{1,0:T(8,128)}, f32[392,384]{1,0:T(8,128)S(1)}, u32[]{:S(2)}, u32[]{:S(2)}) collective-permute-start(f32[392,384]{1,0:T(8,128)} %get-tuple-element.45), channel_id=1, source_target_pairs={{0,2},{1,9},{2,0},{3,11},{4,6},{5,13},{6,4},{7,15},{8,10},{9,1},{1... | collective-permute-start | bytes 1806344 | tf_op jit(solution)/shard_map/ppermute | solution.py:209
  140.9 8.2 %collective-permute-start.15 = (f32[200,384]{1,0:T(8,128)}, f32[200,384]{1,0:T(8,128)S(1)}, u32[]{:S(2)}, u32[]{:S(2)}) collective-permute-start(f32[200,384]{1,0:T(8,128)} %get-tuple-element.47), channel_id=1, source_target_pairs={{0,4},{1,3},{2,6},{3,1},{4,0},{5,7},{6,2},{7,5},{8,12},{9,11},{10,... | collective-permute-start | bytes 921608 | tf_op jit(solution)/shard_map/ppermute | solution.py:209
  151.7 5.5 %collective-permute-start.16 = (f32[104,384]{1,0:T(8,128)}, f32[104,384]{1,0:T(8,128)S(1)}, u32[]{:S(2)}, u32[]{:S(2)}) collective-permute-start(f32[104,384]{1,0:T(8,128)} %get-tuple-element.49), channel_id=1, source_target_pairs={{0,8},{1,5},{2,10},{3,7},{4,12},{5,1},{6,14},{7,3},{8,0},{9,13},{1... | collective-permute-start | bytes 479240 | tf_op jit(solution)/shard_map/ppermute | solution.py:209
  158.1 8.2 %collective-permute-start.17 = (f32[104,384]{1,0:T(8,128)S(1)}, f32[104,384]{1,0:T(8,128)S(1)}, u32[]{:S(2)}, u32[]{:S(2)}) collective-permute-start(f32[104,384]{1,0:T(8,128)S(1)} %add.20.mine_ref), channel_id=1, source_target_pairs={{0,16},{1,17},{2,18},{3,19},{4,20},{5,21},{6,22},{7,23},{8,24},{9,... | collective-permute-start | bytes 479240 | tf_op jit(solution)/shard_map/ppermute | solution.py:209
  168.9 5.9 %collective-permute-start.18 = (f32[96,384]{1,0:T(8,128)}, f32[96,384]{1,0:T(8,128)S(1)}, u32[]{:S(2)}, u32[]{:S(2)}) collective-permute-start(f32[96,384]{1,0:T(8,128)} %get-tuple-element.51), channel_id=1, source_target_pairs={{0,8},{1,5},{2,10},{3,7},{4,12},{5,1},{6,14},{7,3},{8,0},{9,13},{1... | collective-permute-start | bytes 442376 | tf_op jit(solution)/shard_map/ppermute | solution.py:209
  175.8 6.8 %collective-permute-start.19 = (f32[192,384]{1,0:T(8,128)S(1)}, f32[192,384]{1,0:T(8,128)S(1)}, u32[]{:S(2)}, u32[]{:S(2)}) collective-permute-start(f32[192,384]{1,0:T(8,128)S(1)} %maximum_select_fusion.1), channel_id=1, source_target_pairs={{0,4},{1,9},{2,6},{3,11},{4,0},{5,13},{6,2},{7,15},{8,12},{9,1},{1... | collective-permute-start | bytes 884744 | tf_op jit(solution)/shard_map/ppermute | solution.py:209
  (22 other events, 41.0 us)

commit v2 on v0

v2 whole, which is shorter than its diff:
```python
import functools

import jax
import jax.numpy as jnp
from jax import lax
from jax.experimental import pallas as pl
from jax.experimental.pallas import tpu as pltpu
from jax.sharding import PartitionSpec as P


ITERS = 2
AXES = ("term", "sector")
TILE = (8, 128)
CHUNKS = 2

epsilon = 1e-06


VMEM = pl.BlockSpec(memory_space=pltpu.VMEM)
SMEM = pl.BlockSpec(memory_space=pltpu.SMEM)
F32 = jnp.float32
BF16 = jnp.bfloat16

DIMS = (("sector", 1), ("term", 0), ("term", 1))
CORE = ("sector", 0)
ORDERS = ((0, 1, 2), (2, 0, 1))


def matmul_cost(pairs, rows, b):
    return pl.CostEstimate(
        flops=6 * pairs * rows * b * b, bytes_accessed=8 * pairs * b * b, transcendentals=0
    )


def grant(mib):
    return pltpu.CompilerParams(vmem_limit_bytes=mib << 20)


def bit_of(axis, bit):
    return (lax.axis_index(axis) >> bit) & 1


def place(bits, parity, rows):
    return 2 * bits[0] + parity, pl.multiple_of((2 * bits[1] + bits[2]) * rows, 8)


def piece_place(k, parity, rows):
    return place([bit_of(*dim) ^ ((k >> (2 - i)) & 1) for i, dim in enumerate(DIMS)], parity, rows)


def slot_bits(j, order):
    flip = [0, 0, 0]
    for i, dim in enumerate(order):
        flip[dim] = (j >> (2 - i)) & 1
    return flip


def slot_place(j, parity, rows):
    a, b = slot_bits(j, ORDERS[0]), slot_bits(j, ORDERS[1])
    flip = [x if x == y else jnp.where(parity == 0, x, y) for x, y in zip(a, b)]
    return place([bit_of(*dim) ^ f for dim, f in zip(DIMS, flip)], parity, rows)


def split(x):
    high = x.astype(BF16)
    return high, (x - high.astype(F32)).astype(BF16)


def prep_kernel(left_ref, right_ref, psi_ref, diag_ref, lh_ref, ll_ref, rh_ref, rl_ref, vec_ref, mine_ref):
    def one(p, carry):
        lh_ref[p], ll_ref[p] = split(left_ref[p])
        rh_ref[p], rl_ref[p] = split(right_ref[p])
        return carry

    lax.fori_loop(0, left_ref.shape[0], one, 0)
    rows = vec_ref.shape[0] // CHUNKS
    for h in range(CHUNKS):
        _, row = piece_place(0, 0, rows)
        at = pl.ds(pl.multiple_of(row + h * 4 * rows, 8), rows)
        vec_ref[h * rows:(h + 1) * rows, :] = psi_ref[0, at, :]
        mine_ref[h * rows:(h + 1) * rows, :] = diag_ref[0, at, :]


def prepare(left_ops, right_ops, psi, diag):
    b = psi.shape[-1]
    shard = jax.ShapeDtypeStruct((b // 4, b), F32)
    return pl.pallas_call(
        prep_kernel,
        in_specs=[VMEM] * 4,
        out_specs=[VMEM] * 6,
        out_shape=[jax.ShapeDtypeStruct(left_ops.shape, BF16)] * 4 + [shard] * 2,
        compiler_params=grant(16),
        cost_estimate=pl.CostEstimate(
            flops=4 * left_ops.size, bytes_accessed=16 * left_ops.size, transcendentals=0
        ),
    )(left_ops, right_ops, psi, diag)


def store_wide(dest, start, x):
    rows = x.shape[0]
    for c in range(x.shape[1] // TILE[1]):
        dest[start + c * rows:start + (c + 1) * rows, :] = x[:, c * TILE[1]:(c + 1) * TILE[1]]


DOT_NT = functools.partial(
    lax.dot_general, dimension_numbers=(((1,), (1,)), ((), ())), preferred_element_type=F32
)
DOT = functools.partial(jnp.dot, preferred_element_type=F32)


def inner_kernel(first, cells, pieces, *refs):
    in_ref, count_ref, *refs = refs
    parts = refs[:pieces]
    rh, rl, th_ref, tl_ref, inv_ref, vh, vl = refs[pieces:]
    _, b, _ = vh.shape
    me = lax.axis_index("sector")
    core = me & 1
    total = jnp.zeros((1, b), F32)
    for number, piece in enumerate(parts):
        x = piece[...]
        high, low = split(x)
        total += jnp.sum(x * x, axis=0, keepdims=True)
        if first:
            vh[me ^ number] = high
            vl[me ^ number] = low
        else:
            rows = piece.shape[0] // CHUNKS
            sector, row = piece_place(number >> 1, core ^ (number & 1), rows)
            for h in range(CHUNKS):
                at = pl.ds(pl.multiple_of(row + h * 4 * rows, 8), rows)
                vh[sector, at, :] = high[h * rows:(h + 1) * rows, :]
                vl[sector, at, :] = low[h * rows:(h + 1) * rows, :]
    inv_ref[...] = lax.rsqrt(
        jnp.broadcast_to(jnp.sum(total, axis=1, keepdims=True), (TILE[0], b)) / cells + epsilon
    )

    def one_pair(p, carry):
        source = in_ref[0, p]
        x_h, x_l = vh[source], vl[source]
        r_h, r_l = rh[p], rl[p]
        th_ref[p], tl_ref[p] = split(DOT_NT(x_h, r_h) + (DOT_NT(x_h, r_l) + DOT_NT(x_l, r_h)))
        return carry

    lax.fori_loop(0, count_ref[0], one_pair, 0)


def inner(first, cells, sectors, pair_in, pair_count, pieces, ops):
    pairs, b, _ = ops[0].shape
    half = jax.ShapeDtypeStruct(ops[0].shape, BF16)
    return pl.pallas_call(
        functools.partial(inner_kernel, first, cells, len(pieces)),
        in_specs=[SMEM] * 2 + [VMEM] * (len(pieces) + 2),
        out_specs=[VMEM] * 3,
        out_shape=[half, half, jax.ShapeDtypeStruct((TILE[0], b), F32)],
        scratch_shapes=[pltpu.VMEM((sectors, b, b), BF16), pltpu.VMEM((sectors, b, b), BF16)],
        compiler_params=grant(16),
        cost_estimate=matmul_cost(pairs, b, b),
    )(pair_in, pair_count, *pieces, *ops)


def outer_kernel(first, chunk, cells, pieces, *refs):
    out_ref, count_ref, *refs = refs
    parts = refs[:pieces]
    lh, ll, th, tl, inv_ref, before_ref, send_ref, keep_ref, rho_ref, acc = refs[pieces:]
    _, rows, b = acc.shape
    shard = rows // 4
    core = lax.axis_index("sector") & 1
    acc[...] = jnp.zeros_like(acc)
    here = slice(chunk * rows, (chunk + 1) * rows)

    def one_pair(p, carry):
        target = out_ref[0, p]
        l_h, l_l = lh[p, here, :], ll[p, here, :]
        t_h, t_l = th[p], tl[p]
        acc[target] += DOT(l_h, t_h) + (DOT(l_h, t_l) + DOT(l_l, t_h))
        return carry

    lax.fori_loop(0, count_ref[0], one_pair, 0)
    scale = inv_ref[:1, :]
    rho = jnp.zeros((1, b), F32)
    wide = shard * b // TILE[1]
    for number in range(16):
        k, parity = number >> 1, core ^ (number & 1)
        sector, row = piece_place(k, parity, shard)
        x = acc[sector, pl.ds(row, shard), :] * scale
        if first:
            part = parts[(k >> 2) * 2 + (number & 1)]
            v = part[pl.ds(pl.multiple_of(row + chunk * rows, 8), shard), :]
        else:
            v = parts[number][chunk * shard:(chunk + 1) * shard, :]
        rho += jnp.sum(x * v, axis=0, keepdims=True)
    for dest, parity in ((send_ref, 1 - core), (keep_ref, core)):
        for j in range(8):
            sector, row = slot_place(j, parity, shard)
            store_wide(dest, j * wide, acc[sector, pl.ds(row, shard), :] * scale)
    rho = jnp.broadcast_to(jnp.sum(rho * scale, axis=1, keepdims=True), TILE) / cells + before_ref[...]
    rho_ref[...] = rho
    if chunk == CHUNKS - 1:
        send_ref[8 * wide:, :] = rho
        keep_ref[8 * wide:, :] = rho


def outer(first, chunk, cells, sectors, pair_out, pair_count, pieces, ops, inv, before):
    pairs, b, _ = ops[0].shape
    rows = b // CHUNKS
    extra = TILE[0] if chunk == CHUNKS - 1 else 0
    half = jax.ShapeDtypeStruct((sectors * rows // 2 * b // TILE[1] + extra, TILE[1]), F32)
    return pl.pallas_call(
        functools.partial(outer_kernel, first, chunk, cells, len(pieces)),
        in_specs=[SMEM] * 2 + [VMEM] * (len(pieces) + 6),
        out_specs=[VMEM] * 3,
        out_shape=[half, half, jax.ShapeDtypeStruct(TILE, F32)],
        scratch_shapes=[pltpu.VMEM((sectors, rows, b), F32)],
        compiler_params=grant(20),
        cost_estimate=matmul_cost(pairs, rows, b),
    )(pair_out, pair_count, *pieces, *ops, inv, before)


def combine_kernel(keep_ref, recv_ref, next_ref, send_ref=None):
    extra = 0 if send_ref is None else 2 * next_ref.shape[0] - keep_ref.shape[0]
    rows = next_ref.shape[0] - extra
    next_ref[:rows, :] = keep_ref[:rows, :] + recv_ref[:rows, :]
    if send_ref is None:
        return
    send_ref[:rows, :] = keep_ref[rows:2 * rows, :] + recv_ref[rows:2 * rows, :]
    if extra:
        total = keep_ref[2 * rows:, :] + recv_ref[2 * rows:, :]
        next_ref[rows:, :] = total
        send_ref[rows:, :] = total


def combine(keep, recv, extra):
    shape = jax.ShapeDtypeStruct(((keep.shape[0] - extra) // 2 + extra, TILE[1]), F32)
    return pl.pallas_call(
        combine_kernel,
        in_specs=[VMEM] * 2,
        out_specs=[VMEM] * 2,
        out_shape=[shape] * 2,
        compiler_params=grant(4),
    )(keep, recv)


def total(mine, recv):
    return pl.pallas_call(
        combine_kernel,
        in_specs=[VMEM] * 2,
        out_specs=VMEM,
        out_shape=jax.ShapeDtypeStruct(mine.shape, F32),
        compiler_params=grant(4),
    )(mine, recv)


def update_kernel(*refs):
    sums, (vec_ref, inv_ref, diag_ref, new_ref, energy_ref) = refs[:2 * CHUNKS], refs[2 * CHUNKS:]
    rows, b = new_ref.shape
    shard = rows // CHUNKS
    end = shard * b // TILE[1]
    rho = sums[-2][end:, :] + sums[-1][end:, :]
    energy_ref[...] = rho
    for h in range(CHUNKS):
        mine_ref, recv_ref = sums[2 * h:2 * h + 2]
        at = slice(h * shard, (h + 1) * shard)
        for c in range(b // TILE[1]):
            part = slice(c * shard, (c + 1) * shard)
            lanes = slice(c * TILE[1], (c + 1) * TILE[1])
            normed = vec_ref[at, lanes] * inv_ref[:1, lanes]
            sigma = mine_ref[part, :] + recv_ref[part, :]
            residual = sigma - rho[:1, :] * normed
            gap = jnp.maximum(jnp.abs(diag_ref[at, lanes] - rho[:1, :]), 1.0)
            new_ref[at, lanes] = normed - residual / gap


def update(sums, vec, inv, diag):
    return pl.pallas_call(
        update_kernel,
        in_specs=[VMEM] * (len(sums) + 3),
        out_specs=[VMEM] * 2,
        out_shape=[jax.ShapeDtypeStruct(vec.shape, F32), jax.ShapeDtypeStruct(TILE, F32)],
        compiler_params=grant(4),
    )(*sums, vec, inv, diag)


def join_kernel(*refs):
    *parts, out_ref = refs
    rows = parts[0].shape[0] // CHUNKS
    for k, part in enumerate(parts):
        _, row = piece_place(k, 0, rows)
        for h in range(CHUNKS):
            at = pl.ds(pl.multiple_of(row + h * 4 * rows, 8), rows)
            out_ref[0, at, :] = part[h * rows:(h + 1) * rows, :]


def join(parts):
    quarter, b = parts[0].shape
    return pl.pallas_call(
        join_kernel,
        in_specs=[VMEM] * len(parts),
        out_specs=VMEM,
        out_shape=jax.ShapeDtypeStruct((1, 4 * quarter, b), F32),
        compiler_params=grant(4),
    )(*parts)


def flips(mesh_shape, even, odd):
    terms, sectors = mesh_shape
    pairs = []
    for t in range(terms):
        for s in range(sectors):
            u = {"term": t, "sector": s}
            for axis, bit in odd if s & 1 else even:
                u[axis] ^= 1 << bit
            pairs.append((t * sectors + s, u["term"] * sectors + u["sector"]))
    return pairs


def rest_dims(terms):
    return [("term", bit) for bit in range(2, terms.bit_length() - 1)]


def shards(mesh_shape, psi_start, diagonal, left_ops, right_ops, pair_in, pair_out, pair_count):
    terms, sectors = mesh_shape
    b = psi_start.shape[1]
    cells = float(sectors * b * b)

    def swap(x, even, odd=None):
        return lax.ppermute(x, AXES, flips(mesh_shape, even, even if odd is None else odd))

    def dims_of(k):
        return [dim for i, dim in enumerate(DIMS) if (k >> (2 - i)) & 1]

    away = sorted(range(1, 8), key=lambda k: -len(dims_of(k)))
    rest = rest_dims(terms)

    own = psi_start[0]
    across = swap(own, [DIMS[0]])
    beside = swap(own, [CORE])
    lh, ll, rh, rl, vec, diag = prepare(left_ops, right_ops, psi_start, diagonal)
    across, lh, ll, rh, rl, vec, diag = lax.optimization_barrier((across, lh, ll, rh, rl, vec, diag))
    corner = swap(across, [CORE])
    pieces = (own, beside, across, corner)
    energies = []
    for sweep in range(ITERS):
        first = sweep == 0
        th, tl, inv = inner(first, cells, sectors, pair_in, pair_count, pieces, (rh, rl))
        rho = jnp.zeros(TILE, F32)
        keeps, recvs = [], []
        for h in range(CHUNKS):
            send, keep, rho = outer(
                first, h, cells, sectors, pair_out, pair_count, pieces, (lh, ll, th, tl), inv, rho
            )
            keeps.append(keep)
            recvs.append(swap(send, [CORE]))
        for step in zip(*ORDERS):
            for h in range(CHUNKS):
                extra = TILE[0] if h == CHUNKS - 1 else 0
                keeps[h], send = combine(keeps[h], recvs[h], extra)
                recvs[h] = swap(send, [DIMS[step[0]]], [DIMS[step[1]]])
        for step in rest:
            for h in range(CHUNKS):
                keeps[h] = total(keeps[h], recvs[h])
                recvs[h] = swap(keeps[h], [step])
        sums = [x for pair in zip(keeps, recvs) for x in pair]
        vec, energy = update(sums, vec, inv, diag)
        energies.append(energy[0, 0])
        if sweep < ITERS - 1:
            got = {k: swap(vec, dims_of(k)) for k in away}
            got[0] = vec
            pieces = []
            for k in range(8):
                pieces += [got[k], swap(got[k], [CORE])]
    got = {k: swap(vec, dims_of(k)) for k in (3, 2, 1)}
    block = join([vec, got[1], got[2], got[3]])
    return block, jnp.stack(energies)


def solution(mesh):
    mesh_shape = (mesh.shape["term"], mesh.shape["sector"])
    return jax.shard_map(
        functools.partial(shards, mesh_shape),
        mesh=mesh,
        in_specs=(
            P("sector", None, None),
            P("sector", None, None),
            P(("term", "sector"), None, None),
            P(("term", "sector"), None, None),
            P(("term", "sector"), None),
            P(("term", "sector"), None),
            P(("term", "sector")),
        ),
        out_specs=(P("sector", None, None), P()),
        check_vma=False,
    )
```

time: 409 us -> 134 us (0.33)
  waiting for transfers between devices: 266 us -> 59.3 us
  starting transfers between devices: 0.24 us -> 41.3 us
  matrix products: 38.7 us -> 0 us
  loops' own time: 35.8 us -> 0 us
  blocking collectives: 28.7 us -> 0 us
  Pallas kernels: 0 us -> 22.8 us
  between operations: 16.9 us -> 1.5 us
  other arithmetic: 12.8 us -> 1.91 us
    psum x2 -> x0, waiting for transfers between devices: 153 us -> none  [sigma_blocks(): return lax.psum(owned_sum, 'term')]
    reduce_scatter x2 -> x0, waiting for transfers between devices: 65.6 us -> none  [sigma_blocks(): lax.psum_scatter(partial_value, 'sector', scatter_dimension=0, tiled=True)]
    ppermute x0 -> x41, waiting for transfers between devices: none -> 59.3 us  [swap(): lax.ppermute(x, AXES, flips(mesh_shape, even, even if odd is None else odd))]
    all_gather x2 -> x0, waiting for transfers between devices: 47 us -> none  [sigma_blocks(): gathered = lax.all_gather(vector, 'sector', axis=0, tiled=True)]
    ppermute x0 -> x41, starting transfers between devices: none -> 41.3 us  [swap(): lax.ppermute(x, AXES, flips(mesh_shape, even, even if odd is None else odd))]
    dot_general x16 -> x0, matrix products: 38.7 us -> none  [the longest x8 20 us: one_pair(): inner_prod = jnp.dot(left_block, source, precision=lax.Precision.HIGHEST)]
    another operation x2 -> x0, loops' own time: 35.8 us -> none  [apply_pairs(): lax.fori_loop(0, pair_count[0], one_pair, jnp.zeros(gathered.shape, jnp.f...]
    psum x4 -> x0, blocking collectives: 28.7 us -> none  [global_sums(): return lax.psum((values[0],), 'sector')]
  transfers between devices with their start and end apart: 6 -> 41, of which waited for: 6 -> 27; matrix products, arithmetic and copies ran while one was open for 0% -> 2% of each run, Pallas kernels for 0% -> 1%
where the time goes in v2:
time: 134 us; the launch traced here: 133 us
  waiting for transfers between devices  59.3 us (44%)
  starting transfers between devices  41.3 us (31%)
  Pallas kernels  22.8 us (17%)
  local copies, waits for them, and re-layouts  6.6 us (5%)
  other arithmetic  1.91 us (1%)
  between operations  1.5 us (1%)
    ppermute x41, waiting for transfers between devices, swap(): lax.ppermute(x, AXES, flips(mesh_shape, even, even if odd is None else odd))  59.3 us
    ppermute x41, starting transfers between devices, swap(): lax.ppermute(x, AXES, flips(mesh_shape, even, even if odd is None else odd))  41.3 us
    pallas_call x4, Pallas kernels, outer(): pl.pallas_call(functools.partial(outer_kernel, first, chunk, cells, len(p...  11.7 us
    pallas_call x2, Pallas kernels, inner(): pl.pallas_call(functools.partial(inner_kernel, first, cells, len(pieces))...  8.61 us
    unnamed x14, local copies, waits for them, and re-layouts  5.5 us
  transfers between devices with their start and end apart: 41, of which 27 were waited for; matrix products, arithmetic and copies ran while one was open for 2% of the time, Pallas kernels for 1%

profile of v2, /device:TPU:0, one launch (start us, length us, event | category | flops | bytes accessed | tf_op | source)
XLA Modules:
  0.0 133.3 jit_solution(17799125413884007498)
XLA Ops:
  0.6 3.1 %collective-permute-start.1 = (f32[384,384]{1,0:T(8,128)}, f32[384,384]{1,0:T(8,128)S(1)}, u32[]{:S(2)}, u32[]{:S(2)}) collective-permute-start(f32[384,384]{1,0:T(8,128)} %bitcast.3), channel_id=1, source_target_pairs={{0,2},{1,3},{2,0},{3,1},{4,6},{5,7},{6,4},{7,5},{8,10},{9,11},{10,... | collective-permute-start | bytes 1769480 | tf_op jit(solution)/shard_map/ppermute | solution.py:326
  10.1 7.1 %collective-permute-done.1.refs_4_ = f32[384,384]{1,0:T(8,128)S(1)} collective-permute-done((f32[384,384]{1,0:T(8,128)}, f32[384,384]{1,0:T(8,128)S(1)}, u32[]{:S(2)}, u32[]{:S(2)}) %collective-permute-start.1) | collective-permute-done | bytes 589856 | tf_op jit(solution)/shard_map/ppermute | solution.py:326
  19.2 4.4 %shard_map.87 = (bf16[4,384,384]{2,1,0:T(8,128)(2,1)S(1)}, bf16[4,384,384]{2,1,0:T(8,128)(2,1)S(1)}, f32[8,384]{1,0:T(8,128)S(1)}) custom-call(s32[1,4]{1,0:T(1,128)S(1)} %copy-done.6, s32[1]{0:T(128)S(6)} %copy.9.refs_1_, f32[384,384]{1,0:T(8,128)S(1)} %bitcast.5, f32[384,384]{1,0:T(8,128)S(1)} %collective-permute-done.refs_3_, ...), custom_call_target="tpu_custom_call" | custom-call | flops 1358954496 | bytes 4718592 | tf_op jit(solution)/shard_map/pallas_call | solution.py:150
  23.7 2.6 %shard_map.88 = (f32[1152,128]{1,0:T(8,128)S(1)}, f32[1152,128]{1,0:T(8,128)S(1)}, f32[8,128]{1,0:T(8,128)S(1)}) custom-call(s32[1,4]{1,0:T(1,128)S(1)} %copy-done.5, s32[1]{0:T(128)S(6)} %copy.9.refs_1_, f32[384,384]{1,0:T(8,128)S(1)} %bitcast.6, f32[384,384]{1,0:T(8,128)S(1)} %collective-permute-done.refs_3_, ...), custom_call_target="tpu_custom_call" | custom-call | flops 679477248 | bytes 4718592 | tf_op jit(solution)/shard_map/pallas_call | solution.py:208
  26.3 3.2 %shard_map.93 = (f32[1160,128]{1,0:T(8,128)S(1)}, f32[1160,128]{1,0:T(8,128)S(1)}, f32[8,128]{1,0:T(8,128)}) custom-call(s32[1,4]{1,0:T(1,128)S(1)} %copy-done.5, s32[1]{0:T(128)S(6)} %copy.9.refs_1_, f32[384,384]{1,0:T(8,128)S(1)} %bitcast.7, f32[384,384]{1,0:T(8,128)S(1)} %collective-permute-done.refs_3_, f32[384,384]{1,0:T(8,128)S(1)} %collective-permute-done.1.refs_4_, ...), custom_call_target="tpu_custom_call" | custom-call | flops 679477248 | bytes 4718592 | tf_op jit(solution)/shard_map/pallas_call | solution.py:208
  33.8 4.6 %collective-permute-done.9.recv_ref = f32[584,128]{1,0:T(8,128)S(1)} collective-permute-done((f32[584,128]{1,0:T(8,128)S(1)}, f32[584,128]{1,0:T(8,128)S(1)}, u32[]{:S(2)}, u32[]{:S(2)}) %collective-permute-start.9) | collective-permute-done | bytes 299040 | tf_op jit(solution)/shard_map/ppermute | solution.py:326
  38.5 4.2 %collective-permute-done.4.recv_ref = f32[576,128]{1,0:T(8,128)S(1)} collective-permute-done((f32[576,128]{1,0:T(8,128)S(1)}, f32[576,128]{1,0:T(8,128)S(1)}, u32[]{:S(2)}, u32[]{:S(2)}) %collective-permute-start.4) | collective-permute-done | bytes 294944 | tf_op jit(solution)/shard_map/ppermute | solution.py:326
  45.8 3.3 %collective-permute-done.5.recv_ref = f32[288,128]{1,0:T(8,128)S(1)} collective-permute-done((f32[288,128]{1,0:T(8,128)S(1)}, f32[288,128]{1,0:T(8,128)S(1)}, u32[]{:S(2)}, u32[]{:S(2)}) %collective-permute-start.5) | collective-permute-done | bytes 147488 | tf_op jit(solution)/shard_map/ppermute | solution.py:326
  50.6 3.1 %collective-permute-start.12 = (f32[152,128]{1,0:T(8,128)S(1)}, f32[152,128]{1,0:T(8,128)S(1)}, u32[]{:S(2)}, u32[]{:S(2)}) collective-permute-start(f32[152,128]{1,0:T(8,128)S(1)} %shard_map.97.refs_2_), channel_id=1, source_target_pairs={{0,16},{1,17},{2,18},{3,19},{4,20},{5,21},{6,22},{7,23},{8,24},{9,... | collective-permute-start | bytes 233480 | tf_op jit(solution)/shard_map/ppermute | solution.py:326
  54.3 2.9 %collective-permute-start.7 = (f32[144,128]{1,0:T(8,128)S(1)}, f32[144,128]{1,0:T(8,128)S(1)}, u32[]{:S(2)}, u32[]{:S(2)}) collective-permute-start(f32[144,128]{1,0:T(8,128)S(1)} %shard_map.92.refs_0_), channel_id=1, source_target_pairs={{0,16},{1,17},{2,18},{3,19},{4,20},{5,21},{6,22},{7,23},{8,24},{9,... | collective-permute-start | bytes 221192 | tf_op jit(solution)/shard_map/ppermute | solution.py:326
  59.8 2.5 %collective-permute-start.14 = (f32[96,384]{1,0:T(8,128)S(1)}, f32[96,384]{1,0:T(8,128)S(1)}, u32[]{:S(2)}, u32[]{:S(2)}) collective-permute-start(f32[96,384]{1,0:T(8,128)S(1)} %get-tuple-element.92.refs_2_.refs_4_), channel_id=1, source_target_pairs={{0,8},{1,9},{2,10},{3,11},{4,12},{5,13},{6,14},{7,15},{8,0},{9,1},... | collective-permute-start | bytes 442376 | tf_op jit(solution)/shard_map/ppermute | solution.py:326
  64.6 2.6 %collective-permute-start.22 = (f32[96,384]{1,0:T(8,128)S(1)}, f32[96,384]{1,0:T(8,128)S(1)}, u32[]{:S(2)}, u32[]{:S(2)}) collective-permute-start(f32[96,384]{1,0:T(8,128)S(1)} %get-tuple-element.92.refs_2_.refs_4_), channel_id=1, source_target_pairs={{0,10},{1,11},{2,8},{3,9},{4,14},{5,15},{6,12},{7,13},{8,2},{9,3},... | collective-permute-start | bytes 442376 | tf_op jit(solution)/shard_map/ppermute | solution.py:326
  69.0 2.8 %collective-permute-done.16.refs_6_ = f32[96,384]{1,0:T(8,128)S(1)} collective-permute-done((f32[96,384]{1,0:T(8,128)S(1)}, f32[96,384]{1,0:T(8,128)S(1)}, u32[]{:S(2)}, u32[]{:S(2)}) %collective-permute-start.16) | collective-permute-done | bytes 147488 | tf_op jit(solution)/shard_map/ppermute | solution.py:326
  72.3 2.9 %collective-permute-done.22.refs_12_ = f32[96,384]{1,0:T(8,128)S(1)} collective-permute-done((f32[96,384]{1,0:T(8,128)S(1)}, f32[96,384]{1,0:T(8,128)S(1)}, u32[]{:S(2)}, u32[]{:S(2)}) %collective-permute-start.22) | collective-permute-done | bytes 147488 | tf_op jit(solution)/shard_map/ppermute | solution.py:326
  75.2 4.5 %collective-permute-done.24.refs_14_ = f32[96,384]{1,0:T(8,128)S(1)} collective-permute-done((f32[96,384]{1,0:T(8,128)S(1)}, f32[96,384]{1,0:T(8,128)S(1)}, u32[]{:S(2)}, u32[]{:S(2)}) %collective-permute-start.24) | collective-permute-done | bytes 147488 | tf_op jit(solution)/shard_map/ppermute | solution.py:326
  81.7 4.2 %shard_map.99 = (bf16[4,384,384]{2,1,0:T(8,128)(2,1)S(1)}, bf16[4,384,384]{2,1,0:T(8,128)(2,1)S(1)}, f32[8,384]{1,0:T(8,128)S(1)}) custom-call(s32[1,4]{1,0:T(1,128)S(1)} %copy-done.6, s32[1]{0:T(128)S(6)} %copy.9.refs_1_, f32[96,384]{1,0:T(8,128)S(1)} %get-tuple-element.92.refs_2_.refs_4_, f32[96,384]{1,0:T(8,128)S(1)} %collective-permute-done.13.refs_3_, ...), custom_call_target="tpu_custom_call" | custom-call | flops 1358954496 | bytes 4718592 | tf_op jit(solution)/shard_map/pallas_call | solution.py:150
  86.0 2.7 %shard_map.100 = (f32[1152,128]{1,0:T(8,128)S(1)}, f32[1152,128]{1,0:T(8,128)S(1)}, f32[8,128]{1,0:T(8,128)S(1)}) custom-call(s32[1,4]{1,0:T(1,128)S(1)} %copy-done.5, s32[1]{0:T(128)S(6)} %copy.9.refs_1_, f32[96,384]{1,0:T(8,128)S(1)} %get-tuple-element.92.refs_2_.refs_4_, f32[96,384]{1,0:T(8,128)S(1)} %collective-permute-done.13.refs_3_, ...), custom_call_target="tpu_custom_call" | custom-call | flops 679477248 | bytes 4718592 | tf_op jit(solution)/shard_map/pallas_call | solution.py:208
  88.6 3.2 %shard_map.105 = (f32[1160,128]{1,0:T(8,128)S(1)}, f32[1160,128]{1,0:T(8,128)S(1)}, f32[8,128]{1,0:T(8,128)}) custom-call(s32[1,4]{1,0:T(1,128)S(1)} %copy-done.5, s32[1]{0:T(128)S(6)} %copy.9.refs_1_, f32[96,384]{1,0:T(8,128)S(1)} %get-tuple-element.92.refs_2_.refs_4_, f32[96,384]{1,0:T(8,128)S(1)} %collective-permute-done.13.refs_3_, ...), custom_call_target="tpu_custom_call" | custom-call | flops 679477248 | bytes 4718592 | tf_op jit(solution)/shard_map/pallas_call | solution.py:208
  96.2 4.6 %collective-permute-done.34.recv_ref = f32[584,128]{1,0:T(8,128)S(1)} collective-permute-done((f32[584,128]{1,0:T(8,128)S(1)}, f32[584,128]{1,0:T(8,128)S(1)}, u32[]{:S(2)}, u32[]{:S(2)}) %collective-permute-start.34) | collective-permute-done | bytes 299040 | tf_op jit(solution)/shard_map/ppermute | solution.py:326
  100.9 4.2 %collective-permute-done.29.recv_ref = f32[576,128]{1,0:T(8,128)S(1)} collective-permute-done((f32[576,128]{1,0:T(8,128)S(1)}, f32[576,128]{1,0:T(8,128)S(1)}, u32[]{:S(2)}, u32[]{:S(2)}) %collective-permute-start.29) | collective-permute-done | bytes 294944 | tf_op jit(solution)/shard_map/ppermute | solution.py:326
  107.9 3.6 %collective-permute-done.30.recv_ref = f32[288,128]{1,0:T(8,128)S(1)} collective-permute-done((f32[288,128]{1,0:T(8,128)S(1)}, f32[288,128]{1,0:T(8,128)S(1)}, u32[]{:S(2)}, u32[]{:S(2)}) %collective-permute-start.30) | collective-permute-done | bytes 147488 | tf_op jit(solution)/shard_map/ppermute | solution.py:326
  112.7 3.5 %collective-permute-start.37 = (f32[152,128]{1,0:T(8,128)S(1)}, f32[152,128]{1,0:T(8,128)S(1)}, u32[]{:S(2)}, u32[]{:S(2)}) collective-permute-start(f32[152,128]{1,0:T(8,128)S(1)} %shard_map.109.refs_2_), channel_id=1, source_target_pairs={{0,16},{1,17},{2,18},{3,19},{4,20},{5,21},{6,22},{7,23},{8,24},{9,... | collective-permute-start | bytes 233480 | tf_op jit(solution)/shard_map/ppermute | solution.py:326
  116.8 2.9 %collective-permute-start.32 = (f32[144,128]{1,0:T(8,128)S(1)}, f32[144,128]{1,0:T(8,128)S(1)}, u32[]{:S(2)}, u32[]{:S(2)}) collective-permute-start(f32[144,128]{1,0:T(8,128)S(1)} %shard_map.104.refs_0_), channel_id=1, source_target_pairs={{0,16},{1,17},{2,18},{3,19},{4,20},{5,21},{6,22},{7,23},{8,24},{9,... | collective-permute-start | bytes 221192 | tf_op jit(solution)/shard_map/ppermute | solution.py:326
  119.7 2.7 %collective-permute-done.32.refs_1_ = f32[144,128]{1,0:T(8,128)S(1)} collective-permute-done((f32[144,128]{1,0:T(8,128)S(1)}, f32[144,128]{1,0:T(8,128)S(1)}, u32[]{:S(2)}, u32[]{:S(2)}) %collective-permute-start.32) | collective-permute-done | bytes 73760 | tf_op jit(solution)/shard_map/ppermute | solution.py:326
  (102 shorter events, 46.5 us)
Async XLA Ops:
  0.6 16.6 %collective-permute-start.1 = (f32[384,384]{1,0:T(8,128)}, f32[384,384]{1,0:T(8,128)S(1)}, u32[]{:S(2)}, u32[]{:S(2)}) collective-permute-start(f32[384,384]{1,0:T(8,128)} %bitcast.3), channel_id=1, source_target_pairs={{0,2},{1,3},{2,0},{3,1},{4,6},{5,7},{6,4},{7,5},{8,10},{9,11},{10,... | collective-permute-start | bytes 1769480 | tf_op jit(solution)/shard_map/ppermute | solution.py:326
  3.7 14.2 %collective-permute-start = (f32[384,384]{1,0:T(8,128)}, f32[384,384]{1,0:T(8,128)S(1)}, u32[]{:S(2)}, u32[]{:S(2)}) collective-permute-start(f32[384,384]{1,0:T(8,128)} %bitcast.4), channel_id=1, source_target_pairs={{0,1},{1,0},{2,3},{3,2},{4,5},{5,4},{6,7},{7,6},{8,9},{9,8},{10,11... | collective-permute-start | bytes 1769480 | tf_op jit(solution)/shard_map/ppermute | solution.py:326
  31.6 6.8 %collective-permute-start.9 = (f32[584,128]{1,0:T(8,128)S(1)}, f32[584,128]{1,0:T(8,128)S(1)}, u32[]{:S(2)}, u32[]{:S(2)}) collective-permute-start(f32[584,128]{1,0:T(8,128)S(1)} %get-tuple-element.85), channel_id=1, source_target_pairs={{0,2},{1,9},{2,0},{3,11},{4,6},{5,13},{6,4},{7,15},{8,10},{9,1},{1... | collective-permute-start | bytes 897032 | tf_op jit(solution)/shard_map/ppermute | solution.py:326
  32.4 10.3 %collective-permute-start.4 = (f32[576,128]{1,0:T(8,128)S(1)}, f32[576,128]{1,0:T(8,128)S(1)}, u32[]{:S(2)}, u32[]{:S(2)}) collective-permute-start(f32[576,128]{1,0:T(8,128)S(1)} %get-tuple-element.76), channel_id=1, source_target_pairs={{0,2},{1,9},{2,0},{3,11},{4,6},{5,13},{6,4},{7,15},{8,10},{9,1},{1... | collective-permute-start | bytes 884744 | tf_op jit(solution)/shard_map/ppermute | solution.py:326
  42.8 6.3 %collective-permute-start.5 = (f32[288,128]{1,0:T(8,128)S(1)}, f32[288,128]{1,0:T(8,128)S(1)}, u32[]{:S(2)}, u32[]{:S(2)}) collective-permute-start(f32[288,128]{1,0:T(8,128)S(1)} %get-tuple-element.78), channel_id=1, source_target_pairs={{0,4},{1,3},{2,6},{3,1},{4,0},{5,7},{6,2},{7,5},{8,12},{9,11},{10,... | collective-permute-start | bytes 442376 | tf_op jit(solution)/shard_map/ppermute | solution.py:326
  43.7 6.9 %collective-permute-start.11 = (f32[152,128]{1,0:T(8,128)S(1)}, f32[152,128]{1,0:T(8,128)S(1)}, u32[]{:S(2)}, u32[]{:S(2)}) collective-permute-start(f32[152,128]{1,0:T(8,128)S(1)} %get-tuple-element.89), channel_id=1, source_target_pairs={{0,8},{1,5},{2,10},{3,7},{4,12},{5,1},{6,14},{7,3},{8,0},{9,13},{1... | collective-permute-start | bytes 233480 | tf_op jit(solution)/shard_map/ppermute | solution.py:326
  50.6 9.0 %collective-permute-start.12 = (f32[152,128]{1,0:T(8,128)S(1)}, f32[152,128]{1,0:T(8,128)S(1)}, u32[]{:S(2)}, u32[]{:S(2)}) collective-permute-start(f32[152,128]{1,0:T(8,128)S(1)} %shard_map.97.refs_2_), channel_id=1, source_target_pairs={{0,16},{1,17},{2,18},{3,19},{4,20},{5,21},{6,22},{7,23},{8,24},{9,... | collective-permute-start | bytes 233480 | tf_op jit(solution)/shard_map/ppermute | solution.py:326
  59.8 7.4 %collective-permute-start.14 = (f32[96,384]{1,0:T(8,128)S(1)}, f32[96,384]{1,0:T(8,128)S(1)}, u32[]{:S(2)}, u32[]{:S(2)}) collective-permute-start(f32[96,384]{1,0:T(8,128)S(1)} %get-tuple-element.92.refs_2_.refs_4_), channel_id=1, source_target_pairs={{0,8},{1,9},{2,10},{3,11},{4,12},{5,13},{6,14},{7,15},{8,0},{9,1},... | collective-permute-start | bytes 442376 | tf_op jit(solution)/shard_map/ppermute | solution.py:326
  62.3 9.5 %collective-permute-start.16 = (f32[96,384]{1,0:T(8,128)S(1)}, f32[96,384]{1,0:T(8,128)S(1)}, u32[]{:S(2)}, u32[]{:S(2)}) collective-permute-start(f32[96,384]{1,0:T(8,128)S(1)} %get-tuple-element.92.refs_2_.refs_4_), channel_id=1, source_target_pairs={{0,4},{1,5},{2,6},{3,7},{4,0},{5,1},{6,2},{7,3},{8,12},{9,13},{10,... | collective-permute-start | bytes 442376 | tf_op jit(solution)/shard_map/ppermute | solution.py:326
  63.8 8.0 %collective-permute-start.18 = (f32[96,384]{1,0:T(8,128)S(1)}, f32[96,384]{1,0:T(8,128)S(1)}, u32[]{:S(2)}, u32[]{:S(2)}) collective-permute-start(f32[96,384]{1,0:T(8,128)S(1)} %get-tuple-element.92.refs_2_.refs_4_), channel_id=1, source_target_pairs={{0,12},{1,13},{2,14},{3,15},{4,8},{5,9},{6,10},{7,11},{8,4},{9,5},... | collective-permute-start | bytes 442376 | tf_op jit(solution)/shard_map/ppermute | solution.py:326
  63.8 8.0 %collective-permute-start.20 = (f32[96,384]{1,0:T(8,128)S(1)}, f32[96,384]{1,0:T(8,128)S(1)}, u32[]{:S(2)}, u32[]{:S(2)}) collective-permute-start(f32[96,384]{1,0:T(8,128)S(1)} %get-tuple-element.92.refs_2_.refs_4_), channel_id=1, source_target_pairs={{0,2},{1,3},{2,0},{3,1},{4,6},{5,7},{6,4},{7,5},{8,10},{9,11},{10,... | collective-permute-start | bytes 442376 | tf_op jit(solution)/shard_map/ppermute | solution.py:326
  64.6 10.5 %collective-permute-start.22 = (f32[96,384]{1,0:T(8,128)S(1)}, f32[96,384]{1,0:T(8,128)S(1)}, u32[]{:S(2)}, u32[]{:S(2)}) collective-permute-start(f32[96,384]{1,0:T(8,128)S(1)} %get-tuple-element.92.refs_2_.refs_4_), channel_id=1, source_target_pairs={{0,10},{1,11},{2,8},{3,9},{4,14},{5,15},{6,12},{7,13},{8,2},{9,3},... | collective-permute-start | bytes 442376 | tf_op jit(solution)/shard_map/ppermute | solution.py:326
  67.2 12.4 %collective-permute-start.24 = (f32[96,384]{1,0:T(8,128)S(1)}, f32[96,384]{1,0:T(8,128)S(1)}, u32[]{:S(2)}, u32[]{:S(2)}) collective-permute-start(f32[96,384]{1,0:T(8,128)S(1)} %get-tuple-element.92.refs_2_.refs_4_), channel_id=1, source_target_pairs={{0,6},{1,7},{2,4},{3,5},{4,2},{5,3},{6,0},{7,1},{8,14},{9,15},{10,... | collective-permute-start | bytes 442376 | tf_op jit(solution)/shard_map/ppermute | solution.py:326
  71.8 7.9 %collective-permute-start.26 = (f32[96,384]{1,0:T(8,128)S(1)}, f32[96,384]{1,0:T(8,128)S(1)}, u32[]{:S(2)}, u32[]{:S(2)}) collective-permute-start(f32[96,384]{1,0:T(8,128)S(1)} %get-tuple-element.92.refs_2_.refs_4_), channel_id=1, source_target_pairs={{0,14},{1,15},{2,12},{3,13},{4,10},{5,11},{6,8},{7,9},{8,6},{9,7},... | collective-permute-start | bytes 442376 | tf_op jit(solution)/shard_map/ppermute | solution.py:326
  71.8 8.4 %collective-permute-start.15 = (f32[96,384]{1,0:T(8,128)S(1)}, f32[96,384]{1,0:T(8,128)S(1)}, u32[]{:S(2)}, u32[]{:S(2)}) collective-permute-start(f32[96,384]{1,0:T(8,128)S(1)} %collective-permute-done.14.refs_4_), channel_id=1, source_target_pairs={{0,1},{1,0},{2,3},{3,2},{4,5},{5,4},{6,7},{7,6},{8,9},{9,8},{10,11... | collective-permute-start | bytes 442376 | tf_op jit(solution)/shard_map/ppermute | solution.py:326
  71.8 8.4 %collective-permute-start.17 = (f32[96,384]{1,0:T(8,128)S(1)}, f32[96,384]{1,0:T(8,128)S(1)}, u32[]{:S(2)}, u32[]{:S(2)}) collective-permute-start(f32[96,384]{1,0:T(8,128)S(1)} %collective-permute-done.16.refs_6_), channel_id=1, source_target_pairs={{0,1},{1,0},{2,3},{3,2},{4,5},{5,4},{6,7},{7,6},{8,9},{9,8},{10,11... | collective-permute-start | bytes 442376 | tf_op jit(solution)/shard_map/ppermute | solution.py:326
  93.9 6.8 %collective-permute-start.34 = (f32[584,128]{1,0:T(8,128)S(1)}, f32[584,128]{1,0:T(8,128)S(1)}, u32[]{:S(2)}, u32[]{:S(2)}) collective-permute-start(f32[584,128]{1,0:T(8,128)S(1)} %get-tuple-element.108), channel_id=1, source_target_pairs={{0,2},{1,9},{2,0},{3,11},{4,6},{5,13},{6,4},{7,15},{8,10},{9,1},{1... | collective-permute-start | bytes 897032 | tf_op jit(solution)/shard_map/ppermute | solution.py:326
  94.8 10.3 %collective-permute-start.29 = (f32[576,128]{1,0:T(8,128)S(1)}, f32[576,128]{1,0:T(8,128)S(1)}, u32[]{:S(2)}, u32[]{:S(2)}) collective-permute-start(f32[576,128]{1,0:T(8,128)S(1)} %get-tuple-element.99), channel_id=1, source_target_pairs={{0,2},{1,9},{2,0},{3,11},{4,6},{5,13},{6,4},{7,15},{8,10},{9,1},{1... | collective-permute-start | bytes 884744 | tf_op jit(solution)/shard_map/ppermute | solution.py:326
  105.1 6.4 %collective-permute-start.30 = (f32[288,128]{1,0:T(8,128)S(1)}, f32[288,128]{1,0:T(8,128)S(1)}, u32[]{:S(2)}, u32[]{:S(2)}) collective-permute-start(f32[288,128]{1,0:T(8,128)S(1)} %get-tuple-element.101), channel_id=1, source_target_pairs={{0,4},{1,3},{2,6},{3,1},{4,0},{5,7},{6,2},{7,5},{8,12},{9,11},{10,... | collective-permute-start | bytes 442376 | tf_op jit(solution)/shard_map/ppermute | solution.py:326
  106.1 6.6 %collective-permute-start.36 = (f32[152,128]{1,0:T(8,128)S(1)}, f32[152,128]{1,0:T(8,128)S(1)}, u32[]{:S(2)}, u32[]{:S(2)}) collective-permute-start(f32[152,128]{1,0:T(8,128)S(1)} %get-tuple-element.112), channel_id=1, source_target_pairs={{0,8},{1,5},{2,10},{3,7},{4,12},{5,1},{6,14},{7,3},{8,0},{9,13},{1... | collective-permute-start | bytes 233480 | tf_op jit(solution)/shard_map/ppermute | solution.py:326
  112.7 9.7 %collective-permute-start.37 = (f32[152,128]{1,0:T(8,128)S(1)}, f32[152,128]{1,0:T(8,128)S(1)}, u32[]{:S(2)}, u32[]{:S(2)}) collective-permute-start(f32[152,128]{1,0:T(8,128)S(1)} %shard_map.109.refs_2_), channel_id=1, source_target_pairs={{0,16},{1,17},{2,18},{3,19},{4,20},{5,21},{6,22},{7,23},{8,24},{9,... | collective-permute-start | bytes 233480 | tf_op jit(solution)/shard_map/ppermute | solution.py:326
  122.5 7.0 %collective-permute-start.38 = (f32[96,384]{1,0:T(8,128)S(1)}, f32[96,384]{1,0:T(8,128)S(1)}, u32[]{:S(2)}, u32[]{:S(2)}) collective-permute-start(f32[96,384]{1,0:T(8,128)S(1)} %get-tuple-element.113.refs_0_), channel_id=1, source_target_pairs={{0,8},{1,9},{2,10},{3,11},{4,12},{5,13},{6,14},{7,15},{8,0},{9,1},... | collective-permute-start | bytes 442376 | tf_op jit(solution)/shard_map/ppermute | solution.py:326
  124.6 6.1 %collective-permute-start.39 = (f32[96,384]{1,0:T(8,128)S(1)}, f32[96,384]{1,0:T(8,128)S(1)}, u32[]{:S(2)}, u32[]{:S(2)}) collective-permute-start(f32[96,384]{1,0:T(8,128)S(1)} %get-tuple-element.113.refs_0_), channel_id=1, source_target_pairs={{0,4},{1,5},{2,6},{3,7},{4,0},{5,1},{6,2},{7,3},{8,12},{9,13},{10,... | collective-permute-start | bytes 442376 | tf_op jit(solution)/shard_map/ppermute | solution.py:326
  126.4 6.0 %collective-permute-start.40 = (f32[96,384]{1,0:T(8,128)S(1)}, f32[96,384]{1,0:T(8,128)S(1)}, u32[]{:S(2)}, u32[]{:S(2)}) collective-permute-start(f32[96,384]{1,0:T(8,128)S(1)} %get-tuple-element.113.refs_0_), channel_id=1, source_target_pairs={{0,12},{1,13},{2,14},{3,15},{4,8},{5,9},{6,10},{7,11},{8,4},{9,5},... | collective-permute-start | bytes 442376 | tf_op jit(solution)/shard_map/ppermute | solution.py:326
  (24 other events, 99.7 us)

commit v3 on v2

--- a/solution.py
+++ b/solution.py
@@ -24,6 +24,7 @@
 DIMS = (("sector", 1), ("term", 0), ("term", 1))
 CORE = ("sector", 0)
 ORDERS = ((0, 1, 2), (2, 0, 1))
+GATHER = ((0, 1, 2), (2, 1, 0))
 
 
 def matmul_cost(pairs, rows, b):
@@ -55,10 +56,26 @@
     return flip
 
 
-def slot_place(j, parity, rows):
-    a, b = slot_bits(j, ORDERS[0]), slot_bits(j, ORDERS[1])
+def slot_place(j, parity, rows, orders=ORDERS):
+    a, b = slot_bits(j, orders[0]), slot_bits(j, orders[1])
     flip = [x if x == y else jnp.where(parity == 0, x, y) for x, y in zip(a, b)]
     return place([bit_of(*dim) ^ f for dim, f in zip(DIMS, flip)], parity, rows)
+
+
+def segments(first, rows, shard):
+    me = lax.axis_index("sector")
+    if first:
+        out = [[(h, me ^ side, h * rows, 0, rows) for h in range(CHUNKS)] for side in range(2)]
+        out += [[(h, me ^ (2 + side), h * rows, 0, rows) for h in range(CHUNKS - 1)] for side in range(2)]
+        for k in range(4):
+            _, row = piece_place(k, 0, shard)
+            out += [[(CHUNKS - 1, me ^ (2 + side), 0, row, shard)] for side in range(2)]
+        return out
+    out = []
+    for number in range(16):
+        sector, row = slot_place(number >> 1, (me & 1) ^ (number & 1), shard, GATHER)
+        out.append([(h, sector, h * shard, row, shard) for h in range(CHUNKS)])
+    return out
 
 
 def split(x):
@@ -113,23 +130,16 @@
     parts = refs[:pieces]
     rh, rl, th_ref, tl_ref, inv_ref, vh, vl = refs[pieces:]
     _, b, _ = vh.shape
-    me = lax.axis_index("sector")
-    core = me & 1
+    rows = b // CHUNKS
     total = jnp.zeros((1, b), F32)
-    for number, piece in enumerate(parts):
-        x = piece[...]
-        high, low = split(x)
-        total += jnp.sum(x * x, axis=0, keepdims=True)
-        if first:
-            vh[me ^ number] = high
-            vl[me ^ number] = low
-        else:
-            rows = piece.shape[0] // CHUNKS
-            sector, row = piece_place(number >> 1, core ^ (number & 1), rows)
-            for h in range(CHUNKS):
-                at = pl.ds(pl.multiple_of(row + h * 4 * rows, 8), rows)
-                vh[sector, at, :] = high[h * rows:(h + 1) * rows, :]
-                vl[sector, at, :] = low[h * rows:(h + 1) * rows, :]
+    for piece, cuts in zip(parts, segments(first, rows, rows // 4)):
+        for chunk, sector, start, row, size in cuts:
+            x = piece[start:start + size, :]
+            high, low = split(x)
+            total += jnp.sum(x * x, axis=0, keepdims=True)
+            at = pl.ds(pl.multiple_of(row + chunk * rows, 16), size)
+            vh[sector, at, :] = high
+            vl[sector, at, :] = low
     inv_ref[...] = lax.rsqrt(
         jnp.broadcast_to(jnp.sum(total, axis=1, keepdims=True), (TILE[0], b)) / cells + epsilon
     )
@@ -179,21 +189,16 @@
     scale = inv_ref[:1, :]
     rho = jnp.zeros((1, b), F32)
     wide = shard * b // TILE[1]
-    for number in range(16):
-        k, parity = number >> 1, core ^ (number & 1)
-        sector, row = piece_place(k, parity, shard)
-        x = acc[sector, pl.ds(row, shard), :] * scale
-        if first:
-            part = parts[(k >> 2) * 2 + (number & 1)]
-            v = part[pl.ds(pl.multiple_of(row + chunk * rows, 8), shard), :]
-        else:
-            v = parts[number][chunk * shard:(chunk + 1) * shard, :]
-        rho += jnp.sum(x * v, axis=0, keepdims=True)
+    for piece, cuts in zip(parts, segments(first, rows, shard)):
+        for at, sector, start, row, size in cuts:
+            if at == chunk:
+                x = acc[sector, pl.ds(row, size), :] * piece[start:start + size, :]
+                rho += jnp.sum(x, axis=0, keepdims=True)
     for dest, parity in ((send_ref, 1 - core), (keep_ref, core)):
         for j in range(8):
             sector, row = slot_place(j, parity, shard)
             store_wide(dest, j * wide, acc[sector, pl.ds(row, shard), :] * scale)
-    rho = jnp.broadcast_to(jnp.sum(rho * scale, axis=1, keepdims=True), TILE) / cells + before_ref[...]
+    rho = jnp.broadcast_to(jnp.sum(rho * scale * scale, axis=1, keepdims=True), TILE) / cells + before_ref[...]
     rho_ref[...] = rho
     if chunk == CHUNKS - 1:
         send_ref[8 * wide:, :] = rho
@@ -280,6 +285,15 @@
     )(*sums, vec, inv, diag)
 
 
+def zero_tile():
+    def kernel(out_ref):
+        out_ref[...] = jnp.zeros_like(out_ref)
+
+    return pl.pallas_call(
+        kernel, out_specs=VMEM, out_shape=jax.ShapeDtypeStruct(TILE, F32), compiler_params=grant(4)
+    )()
+
+
 def join_kernel(*refs):
     *parts, out_ref = refs
     rows = parts[0].shape[0] // CHUNKS
@@ -328,26 +342,33 @@
     def dims_of(k):
         return [dim for i, dim in enumerate(DIMS) if (k >> (2 - i)) & 1]
 
-    away = sorted(range(1, 8), key=lambda k: -len(dims_of(k)))
     rest = rest_dims(terms)
 
     own = psi_start[0]
-    across = swap(own, [DIMS[0]])
+    shard = b // CHUNKS // 4
+    _, row = piece_place(0, 0, shard)
+    share = lax.dynamic_slice(own, (row + (b - b // CHUNKS), 0), (shard, b))
+    share = swap(share, [DIMS[0]])
+    across = swap(own[:b - b // CHUNKS], [DIMS[0]])
     beside = swap(own, [CORE])
+    zero = zero_tile()
     lh, ll, rh, rl, vec, diag = prepare(left_ops, right_ops, psi_start, diagonal)
     across, lh, ll, rh, rl, vec, diag = lax.optimization_barrier((across, lh, ll, rh, rl, vec, diag))
+    shares = [share, swap(share, [DIMS[2]]), swap(share, [DIMS[1]])]
+    last = jnp.where(bit_of(*CORE) == 0, shares[1], shares[2])
+    shares.append(swap(last, [DIMS[1]], [DIMS[2]]))
     corner = swap(across, [CORE])
-    pieces = (own, beside, across, corner)
+    pieces = [own, beside, across, corner]
+    for x in shares:
+        pieces += [x, swap(x, [CORE])]
     energies = []
     for sweep in range(ITERS):
         first = sweep == 0
         th, tl, inv = inner(first, cells, sectors, pair_in, pair_count, pieces, (rh, rl))
-        rho = jnp.zeros(TILE, F32)
+        rho = zero
         keeps, recvs = [], []
         for h in range(CHUNKS):
-            send, keep, rho = outer(
-                first, h, cells, sectors, pair_out, pair_count, pieces, (lh, ll, th, tl), inv, rho
-            )
+            send, keep, rho = outer(first, h, cells, sectors, pair_out, pair_count, pieces, (lh, ll, th, tl), inv, rho)
             keeps.append(keep)
             recvs.append(swap(send, [CORE]))
         for step in zip(*ORDERS):
@@ -363,11 +384,14 @@
         vec, energy = update(sums, vec, inv, diag)
         energies.append(energy[0, 0])
         if sweep < ITERS - 1:
-            got = {k: swap(vec, dims_of(k)) for k in away}
-            got[0] = vec
+            got = [vec] + [None] * 7
+            for j in (1, 2, 4, 3, 5, 6, 7):
+                over = 2 - (j.bit_length() - 1)
+                source = got[j ^ (1 << (2 - over))]
+                got[j] = swap(source, [DIMS[GATHER[0][over]]], [DIMS[GATHER[1][over]]])
             pieces = []
-            for k in range(8):
-                pieces += [got[k], swap(got[k], [CORE])]
+            for x in got:
+                pieces += [x, swap(x, [CORE])]
     got = {k: swap(vec, dims_of(k)) for k in (3, 2, 1)}
     block = join([vec, got[1], got[2], got[3]])
     return block, jnp.stack(energies)

time: 134 us -> 136 us (1.015)
  waiting for transfers between devices: 59.3 us -> 73.8 us
  starting transfers between devices: 41.3 us -> 29 us
    ppermute x41 -> x49, waiting for transfers between devices: 59.3 us -> 73.8 us  [swap(): lax.ppermute(x, AXES, flips(mesh_shape, even, even if odd is None else odd))]
    ppermute x41 -> x49, starting transfers between devices: 41.3 us -> 29 us  [swap(): lax.ppermute(x, AXES, flips(mesh_shape, even, even if odd is None else odd))]
    unnamed x14 -> x12, local copies, waits for them, and re-layouts: 5.5 us -> 4.41 us
  transfers between devices with their start and end apart: 41 -> 49, of which waited for: 27 -> 26; matrix products, arithmetic and copies ran while one was open for 2% -> 3% of each run, Pallas kernels for 1% -> 1%
where the time goes in v3:
time: 136 us
  waiting for transfers between devices  73.8 us (54%)
  starting transfers between devices  29 us (21%)
  Pallas kernels  22.5 us (17%)
  local copies, waits for them, and re-layouts  7.36 us (5%)
  other arithmetic  1.81 us (1%)
  between operations  1.6 us (1%)
    ppermute x49, waiting for transfers between devices, swap(): lax.ppermute(x, AXES, flips(mesh_shape, even, even if odd is None else odd))  73.8 us
    ppermute x49, starting transfers between devices, swap(): lax.ppermute(x, AXES, flips(mesh_shape, even, even if odd is None else odd))  29 us
    pallas_call x4, Pallas kernels, outer(): pl.pallas_call(functools.partial(outer_kernel, first, chunk, cells, len(p...  11.7 us
    pallas_call x2, Pallas kernels, inner(): pl.pallas_call(functools.partial(inner_kernel, first, cells, len(pieces))...  8.36 us
    unnamed x12, local copies, waits for them, and re-layouts  4.41 us
  transfers between devices with their start and end apart: 49, of which 26 were waited for; matrix products, arithmetic and copies ran while one was open for 3% of the time, Pallas kernels for 1%

profile of v3, /device:TPU:0, one launch (start us, length us, event | category | flops | bytes accessed | tf_op | source)
XLA Modules:
  0.0 136.1 jit_solution(5292912185219819369)
XLA Ops:
  1.7 3.1 %collective-permute-start.1 = (f32[192,384]{1,0:T(8,128)S(1)}, f32[192,384]{1,0:T(8,128)S(1)}, u32[]{:S(2)}, u32[]{:S(2)}) collective-permute-start(f32[192,384]{1,0:T(8,128)S(1)} %slice_bitcast_fusion), channel_id=1, source_target_pairs={{0,2},{1,3},{2,0},{3,1},{4,6},{5,7},{6,4},{7,5},{8,10},{9,11},{10,... | collective-permute-start | bytes 884744 | tf_op jit(solution)/shard_map/ppermute | solution.py:340
  5.7 7.6 %collective-permute-done.3.refs_6_ = f32[48,384]{1,0:T(8,128)S(1)} collective-permute-done((f32[48,384]{1,0:T(8,128)S(1)}, f32[48,384]{1,0:T(8,128)S(1)}, u32[]{:S(2)}, u32[]{:S(2)}) %collective-permute-start.3) | collective-permute-done | bytes 73760 | tf_op jit(solution)/shard_map/ppermute | solution.py:340
  23.7 3.3 %collective-permute-done.9.refs_12_ = f32[48,384]{1,0:T(8,128)S(1)} collective-permute-done((f32[48,384]{1,0:T(8,128)S(1)}, f32[48,384]{1,0:T(8,128)S(1)}, u32[]{:S(2)}, u32[]{:S(2)}) %collective-permute-start.9) | collective-permute-done | bytes 73760 | tf_op jit(solution)/shard_map/ppermute | solution.py:340
  28.3 4.3 %shard_map.87 = (bf16[4,384,384]{2,1,0:T(8,128)(2,1)S(1)}, bf16[4,384,384]{2,1,0:T(8,128)(2,1)S(1)}, f32[8,384]{1,0:T(8,128)S(1)}) custom-call(s32[1,4]{1,0:T(1,128)S(1)} %copy-done.5, s32[1]{0:T(128)S(6)} %copy.9.refs_1_, f32[384,384]{1,0:T(8,128)S(1)} %bitcast.8, f32[384,384]{1,0:T(8,128)S(1)} %collective-permute-done.refs_3_, ...), custom_call_target="tpu_custom_call" | custom-call | flops 1358954496 | bytes 4718592 | tf_op jit(solution)/shard_map/pallas_call | solution.py:160
  32.5 2.6 %shard_map.89 = (f32[1152,128]{1,0:T(8,128)S(1)}, f32[1152,128]{1,0:T(8,128)S(1)}, f32[8,128]{1,0:T(8,128)S(1)}) custom-call(s32[1,4]{1,0:T(1,128)S(1)} %copy-done.4, s32[1]{0:T(128)S(6)} %copy.9.refs_1_, f32[384,384]{1,0:T(8,128)S(1)} %bitcast.9, f32[384,384]{1,0:T(8,128)S(1)} %collective-permute-done.refs_3_, ...), custom_call_target="tpu_custom_call" | custom-call | flops 679477248 | bytes 4718592 | tf_op jit(solution)/shard_map/pallas_call | solution.py:213
  35.1 3.2 %shard_map.94 = (f32[1160,128]{1,0:T(8,128)S(1)}, f32[1160,128]{1,0:T(8,128)S(1)}, f32[8,128]{1,0:T(8,128)}) custom-call(s32[1,4]{1,0:T(1,128)S(1)} %copy-done.4, s32[1]{0:T(128)S(6)} %copy.9.refs_1_, f32[384,384]{1,0:T(8,128)S(1)} %bitcast.10, f32[384,384]{1,0:T(8,128)S(1)} %collective-permute-done.refs_3_, f32[192,384]{1,0:T(8,128)S(1)} %collective-permute-done.1.refs_4_, ...), custom_call_target="tpu_custom_call" | custom-call | flops 679477248 | bytes 4718592 | tf_op jit(solution)/shard_map/pallas_call | solution.py:213
  42.6 4.6 %collective-permute-done.17.recv_ref = f32[584,128]{1,0:T(8,128)S(1)} collective-permute-done((f32[584,128]{1,0:T(8,128)S(1)}, f32[584,128]{1,0:T(8,128)S(1)}, u32[]{:S(2)}, u32[]{:S(2)}) %collective-permute-start.17) | collective-permute-done | bytes 299040 | tf_op jit(solution)/shard_map/ppermute | solution.py:340
  47.4 4.2 %collective-permute-done.12.recv_ref = f32[576,128]{1,0:T(8,128)S(1)} collective-permute-done((f32[576,128]{1,0:T(8,128)S(1)}, f32[576,128]{1,0:T(8,128)S(1)}, u32[]{:S(2)}, u32[]{:S(2)}) %collective-permute-start.12) | collective-permute-done | bytes 294944 | tf_op jit(solution)/shard_map/ppermute | solution.py:340
  52.9 5.1 %collective-permute-done.13.recv_ref = f32[288,128]{1,0:T(8,128)S(1)} collective-permute-done((f32[288,128]{1,0:T(8,128)S(1)}, f32[288,128]{1,0:T(8,128)S(1)}, u32[]{:S(2)}, u32[]{:S(2)}) %collective-permute-start.13) | collective-permute-done | bytes 147488 | tf_op jit(solution)/shard_map/ppermute | solution.py:340
  58.1 3.1 %collective-permute-start.20 = (f32[152,128]{1,0:T(8,128)S(1)}, f32[152,128]{1,0:T(8,128)S(1)}, u32[]{:S(2)}, u32[]{:S(2)}) collective-permute-start(f32[152,128]{1,0:T(8,128)S(1)} %shard_map.98.refs_2_), channel_id=1, source_target_pairs={{0,16},{1,17},{2,18},{3,19},{4,20},{5,21},{6,22},{7,23},{8,24},{9,... | collective-permute-start | bytes 233480 | tf_op jit(solution)/shard_map/ppermute | solution.py:340
  64.3 4.5 %collective-permute-done.15.refs_1_ = f32[144,128]{1,0:T(8,128)S(1)} collective-permute-done((f32[144,128]{1,0:T(8,128)S(1)}, f32[144,128]{1,0:T(8,128)S(1)}, u32[]{:S(2)}, u32[]{:S(2)}) %collective-permute-start.15) | collective-permute-done | bytes 73760 | tf_op jit(solution)/shard_map/ppermute | solution.py:340
  70.7 4.8 %collective-permute-done.22.refs_4_ = f32[96,384]{1,0:T(8,128)S(1)} collective-permute-done((f32[96,384]{1,0:T(8,128)S(1)}, f32[96,384]{1,0:T(8,128)S(1)}, u32[]{:S(2)}, u32[]{:S(2)}) %collective-permute-start.22) | collective-permute-done | bytes 147488 | tf_op jit(solution)/shard_map/ppermute | solution.py:340
  78.1 2.6 %collective-permute-done.26.refs_8_ = f32[96,384]{1,0:T(8,128)S(1)} collective-permute-done((f32[96,384]{1,0:T(8,128)S(1)}, f32[96,384]{1,0:T(8,128)S(1)}, u32[]{:S(2)}, u32[]{:S(2)}) %collective-permute-start.26) | collective-permute-done | bytes 147488 | tf_op jit(solution)/shard_map/ppermute | solution.py:340
  82.8 3.0 %collective-permute-done.34.refs_16_ = f32[96,384]{1,0:T(8,128)S(1)} collective-permute-done((f32[96,384]{1,0:T(8,128)S(1)}, f32[96,384]{1,0:T(8,128)S(1)}, u32[]{:S(2)}, u32[]{:S(2)}) %collective-permute-start.34) | collective-permute-done | bytes 147488 | tf_op jit(solution)/shard_map/ppermute | solution.py:340
  87.2 4.1 %shard_map.100 = (bf16[4,384,384]{2,1,0:T(8,128)(2,1)S(1)}, bf16[4,384,384]{2,1,0:T(8,128)(2,1)S(1)}, f32[8,384]{1,0:T(8,128)S(1)}) custom-call(s32[1,4]{1,0:T(1,128)S(1)} %copy-done.5, s32[1]{0:T(128)S(6)} %copy.9.refs_1_, f32[96,384]{1,0:T(8,128)S(1)} %get-tuple-element.92.refs_2_.refs_4_, f32[96,384]{1,0:T(8,128)S(1)} %collective-permute-done.21.refs_3_, ...), custom_call_target="tpu_custom_call" | custom-call | flops 1358954496 | bytes 4718592 | tf_op jit(solution)/shard_map/pallas_call | solution.py:160
  91.3 2.6 %shard_map.101 = (f32[1152,128]{1,0:T(8,128)S(1)}, f32[1152,128]{1,0:T(8,128)S(1)}, f32[8,128]{1,0:T(8,128)S(1)}) custom-call(s32[1,4]{1,0:T(1,128)S(1)} %copy-done.4, s32[1]{0:T(128)S(6)} %copy.9.refs_1_, f32[96,384]{1,0:T(8,128)S(1)} %get-tuple-element.92.refs_2_.refs_4_, f32[96,384]{1,0:T(8,128)S(1)} %collective-permute-done.21.refs_3_, ...), custom_call_target="tpu_custom_call" | custom-call | flops 679477248 | bytes 4718592 | tf_op jit(solution)/shard_map/pallas_call | solution.py:213
  94.0 3.2 %shard_map.106 = (f32[1160,128]{1,0:T(8,128)S(1)}, f32[1160,128]{1,0:T(8,128)S(1)}, f32[8,128]{1,0:T(8,128)}) custom-call(s32[1,4]{1,0:T(1,128)S(1)} %copy-done.4, s32[1]{0:T(128)S(6)} %copy.9.refs_1_, f32[96,384]{1,0:T(8,128)S(1)} %get-tuple-element.92.refs_2_.refs_4_, f32[96,384]{1,0:T(8,128)S(1)} %collective-permute-done.21.refs_3_, ...), custom_call_target="tpu_custom_call" | custom-call | flops 679477248 | bytes 4718592 | tf_op jit(solution)/shard_map/pallas_call | solution.py:213
  101.5 4.6 %collective-permute-done.42.recv_ref = f32[584,128]{1,0:T(8,128)S(1)} collective-permute-done((f32[584,128]{1,0:T(8,128)S(1)}, f32[584,128]{1,0:T(8,128)S(1)}, u32[]{:S(2)}, u32[]{:S(2)}) %collective-permute-start.42) | collective-permute-done | bytes 299040 | tf_op jit(solution)/shard_map/ppermute | solution.py:340
  106.2 4.2 %collective-permute-done.37.recv_ref = f32[576,128]{1,0:T(8,128)S(1)} collective-permute-done((f32[576,128]{1,0:T(8,128)S(1)}, f32[576,128]{1,0:T(8,128)S(1)}, u32[]{:S(2)}, u32[]{:S(2)}) %collective-permute-start.37) | collective-permute-done | bytes 294944 | tf_op jit(solution)/shard_map/ppermute | solution.py:340
  111.5 5.4 %collective-permute-done.38.recv_ref = f32[288,128]{1,0:T(8,128)S(1)} collective-permute-done((f32[288,128]{1,0:T(8,128)S(1)}, f32[288,128]{1,0:T(8,128)S(1)}, u32[]{:S(2)}, u32[]{:S(2)}) %collective-permute-start.38) | collective-permute-done | bytes 147488 | tf_op jit(solution)/shard_map/ppermute | solution.py:340
  117.0 2.7 %collective-permute-start.45 = (f32[152,128]{1,0:T(8,128)S(1)}, f32[152,128]{1,0:T(8,128)S(1)}, u32[]{:S(2)}, u32[]{:S(2)}) collective-permute-start(f32[152,128]{1,0:T(8,128)S(1)} %shard_map.110.refs_2_), channel_id=1, source_target_pairs={{0,16},{1,17},{2,18},{3,19},{4,20},{5,21},{6,22},{7,23},{8,24},{9,... | collective-permute-start | bytes 233480 | tf_op jit(solution)/shard_map/ppermute | solution.py:340
  119.7 2.4 %collective-permute-done.39.recv_ref = f32[144,128]{1,0:T(8,128)S(1)} collective-permute-done((f32[144,128]{1,0:T(8,128)S(1)}, f32[144,128]{1,0:T(8,128)S(1)}, u32[]{:S(2)}, u32[]{:S(2)}) %collective-permute-start.39) | collective-permute-done | bytes 73760 | tf_op jit(solution)/shard_map/ppermute | solution.py:340
  122.7 5.5 %collective-permute-done.40.refs_1_ = f32[144,128]{1,0:T(8,128)S(1)} collective-permute-done((f32[144,128]{1,0:T(8,128)S(1)}, f32[144,128]{1,0:T(8,128)S(1)}, u32[]{:S(2)}, u32[]{:S(2)}) %collective-permute-start.40) | collective-permute-done | bytes 73760 | tf_op jit(solution)/shard_map/ppermute | solution.py:340
  129.1 2.8 %collective-permute-start.48 = (f32[96,384]{1,0:T(8,128)S(1)}, f32[96,384]{1,0:T(8,128)S(1)}, u32[]{:S(2)}, u32[]{:S(2)}) collective-permute-start(f32[96,384]{1,0:T(8,128)S(1)} %get-tuple-element.113.refs_0_), channel_id=1, source_target_pairs={{0,12},{1,13},{2,14},{3,15},{4,8},{5,9},{6,10},{7,11},{8,4},{9,5},... | collective-permute-start | bytes 442376 | tf_op jit(solution)/shard_map/ppermute | solution.py:340
  (119 shorter events, 41.0 us)
Async XLA Ops:
  1.7 20.4 %collective-permute-start.1 = (f32[192,384]{1,0:T(8,128)S(1)}, f32[192,384]{1,0:T(8,128)S(1)}, u32[]{:S(2)}, u32[]{:S(2)}) collective-permute-start(f32[192,384]{1,0:T(8,128)S(1)} %slice_bitcast_fusion), channel_id=1, source_target_pairs={{0,2},{1,3},{2,0},{3,1},{4,6},{5,7},{6,4},{7,5},{8,10},{9,11},{10,... | collective-permute-start | bytes 884744 | tf_op jit(solution)/shard_map/ppermute | solution.py:340
  4.8 23.5 %collective-permute-start = (f32[384,384]{1,0:T(8,128)}, f32[384,384]{1,0:T(8,128)S(1)}, u32[]{:S(2)}, u32[]{:S(2)}) collective-permute-start(f32[384,384]{1,0:T(8,128)} %bitcast.7), channel_id=1, source_target_pairs={{0,1},{1,0},{2,3},{3,2},{4,5},{5,4},{6,7},{7,6},{8,9},{9,8},{10,11... | collective-permute-start | bytes 1769480 | tf_op jit(solution)/shard_map/ppermute | solution.py:340
  5.6 7.7 %collective-permute-start.3 = (f32[48,384]{1,0:T(8,128)S(1)}, f32[48,384]{1,0:T(8,128)S(1)}, u32[]{:S(2)}, u32[]{:S(2)}) collective-permute-start(f32[48,384]{1,0:T(8,128)S(1)} %dynamic-slice_bitcast_fusion), channel_id=1, source_target_pairs={{0,2},{1,3},{2,0},{3,1},{4,6},{5,7},{6,4},{7,5},{8,10},{9,11},{10,... | collective-permute-start | bytes 221192 | tf_op jit(solution)/shard_map/ppermute | solution.py:340
  13.3 9.2 %collective-permute-start.5 = (f32[48,384]{1,0:T(8,128)S(1)}, f32[48,384]{1,0:T(8,128)S(1)}, u32[]{:S(2)}, u32[]{:S(2)}) collective-permute-start(f32[48,384]{1,0:T(8,128)S(1)} %collective-permute-done.3.refs_6_), channel_id=1, source_target_pairs={{0,8},{1,9},{2,10},{3,11},{4,12},{5,13},{6,14},{7,15},{8,0},{9,1},... | collective-permute-start | bytes 221192 | tf_op jit(solution)/shard_map/ppermute | solution.py:340
  15.1 7.4 %collective-permute-start.7 = (f32[48,384]{1,0:T(8,128)S(1)}, f32[48,384]{1,0:T(8,128)S(1)}, u32[]{:S(2)}, u32[]{:S(2)}) collective-permute-start(f32[48,384]{1,0:T(8,128)S(1)} %collective-permute-done.3.refs_6_), channel_id=1, source_target_pairs={{0,4},{1,5},{2,6},{3,7},{4,0},{5,1},{6,2},{7,3},{8,12},{9,13},{10,... | collective-permute-start | bytes 221192 | tf_op jit(solution)/shard_map/ppermute | solution.py:340
  22.0 6.2 %collective-permute-start.2 = (f32[192,384]{1,0:T(8,128)S(1)}, f32[192,384]{1,0:T(8,128)S(1)}, u32[]{:S(2)}, u32[]{:S(2)}) collective-permute-start(f32[192,384]{1,0:T(8,128)S(1)} %collective-permute-done.1.refs_4_), channel_id=1, source_target_pairs={{0,1},{1,0},{2,3},{3,2},{4,5},{5,4},{6,7},{7,6},{8,9},{9,8},{10,11... | collective-permute-start | bytes 884744 | tf_op jit(solution)/shard_map/ppermute | solution.py:340
  40.4 6.8 %collective-permute-start.17 = (f32[584,128]{1,0:T(8,128)S(1)}, f32[584,128]{1,0:T(8,128)S(1)}, u32[]{:S(2)}, u32[]{:S(2)}) collective-permute-start(f32[584,128]{1,0:T(8,128)S(1)} %get-tuple-element.85), channel_id=1, source_target_pairs={{0,2},{1,9},{2,0},{3,11},{4,6},{5,13},{6,4},{7,15},{8,10},{9,1},{1... | collective-permute-start | bytes 897032 | tf_op jit(solution)/shard_map/ppermute | solution.py:340
  41.2 10.3 %collective-permute-start.12 = (f32[576,128]{1,0:T(8,128)S(1)}, f32[576,128]{1,0:T(8,128)S(1)}, u32[]{:S(2)}, u32[]{:S(2)}) collective-permute-start(f32[576,128]{1,0:T(8,128)S(1)} %get-tuple-element.76), channel_id=1, source_target_pairs={{0,2},{1,9},{2,0},{3,11},{4,6},{5,13},{6,4},{7,15},{8,10},{9,1},{1... | collective-permute-start | bytes 884744 | tf_op jit(solution)/shard_map/ppermute | solution.py:340
  51.6 6.4 %collective-permute-start.13 = (f32[288,128]{1,0:T(8,128)S(1)}, f32[288,128]{1,0:T(8,128)S(1)}, u32[]{:S(2)}, u32[]{:S(2)}) collective-permute-start(f32[288,128]{1,0:T(8,128)S(1)} %get-tuple-element.78), channel_id=1, source_target_pairs={{0,4},{1,3},{2,6},{3,1},{4,0},{5,7},{6,2},{7,5},{8,12},{9,11},{10,... | collective-permute-start | bytes 442376 | tf_op jit(solution)/shard_map/ppermute | solution.py:340
  58.1 10.7 %collective-permute-start.20 = (f32[152,128]{1,0:T(8,128)S(1)}, f32[152,128]{1,0:T(8,128)S(1)}, u32[]{:S(2)}, u32[]{:S(2)}) collective-permute-start(f32[152,128]{1,0:T(8,128)S(1)} %shard_map.98.refs_2_), channel_id=1, source_target_pairs={{0,16},{1,17},{2,18},{3,19},{4,20},{5,21},{6,22},{7,23},{8,24},{9,... | collective-permute-start | bytes 233480 | tf_op jit(solution)/shard_map/ppermute | solution.py:340
  63.0 5.8 %collective-permute-start.15 = (f32[144,128]{1,0:T(8,128)S(1)}, f32[144,128]{1,0:T(8,128)S(1)}, u32[]{:S(2)}, u32[]{:S(2)}) collective-permute-start(f32[144,128]{1,0:T(8,128)S(1)} %shard_map.93.refs_0_), channel_id=1, source_target_pairs={{0,16},{1,17},{2,18},{3,19},{4,20},{5,21},{6,22},{7,23},{8,24},{9,... | collective-permute-start | bytes 221192 | tf_op jit(solution)/shard_map/ppermute | solution.py:340
  68.9 6.7 %collective-permute-start.22 = (f32[96,384]{1,0:T(8,128)S(1)}, f32[96,384]{1,0:T(8,128)S(1)}, u32[]{:S(2)}, u32[]{:S(2)}) collective-permute-start(f32[96,384]{1,0:T(8,128)S(1)} %get-tuple-element.92.refs_2_.refs_4_), channel_id=1, source_target_pairs={{0,8},{1,3},{2,10},{3,1},{4,12},{5,7},{6,14},{7,5},{8,0},{9,11},{1... | collective-permute-start | bytes 442376 | tf_op jit(solution)/shard_map/ppermute | solution.py:340
  69.0 6.6 %collective-permute-start.24 = (f32[96,384]{1,0:T(8,128)S(1)}, f32[96,384]{1,0:T(8,128)S(1)}, u32[]{:S(2)}, u32[]{:S(2)}) collective-permute-start(f32[96,384]{1,0:T(8,128)S(1)} %get-tuple-element.92.refs_2_.refs_4_), channel_id=1, source_target_pairs={{0,4},{1,5},{2,6},{3,7},{4,0},{5,1},{6,2},{7,3},{8,12},{9,13},{10,... | collective-permute-start | bytes 442376 | tf_op jit(solution)/shard_map/ppermute | solution.py:340
  69.3 6.8 %collective-permute-start.21 = (f32[96,384]{1,0:T(8,128)S(1)}, f32[96,384]{1,0:T(8,128)S(1)}, u32[]{:S(2)}, u32[]{:S(2)}) collective-permute-start(f32[96,384]{1,0:T(8,128)S(1)} %get-tuple-element.92.refs_2_.refs_4_), channel_id=1, source_target_pairs={{0,1},{1,0},{2,3},{3,2},{4,5},{5,4},{6,7},{7,6},{8,9},{9,8},{10,11... | collective-permute-start | bytes 442376 | tf_op jit(solution)/shard_map/ppermute | solution.py:340
  69.3 7.0 %collective-permute-start.28 = (f32[96,384]{1,0:T(8,128)S(1)}, f32[96,384]{1,0:T(8,128)S(1)}, u32[]{:S(2)}, u32[]{:S(2)}) collective-permute-start(f32[96,384]{1,0:T(8,128)S(1)} %get-tuple-element.92.refs_2_.refs_4_), channel_id=1, source_target_pairs={{0,2},{1,9},{2,0},{3,11},{4,6},{5,13},{6,4},{7,15},{8,10},{9,1},{1... | collective-permute-start | bytes 442376 | tf_op jit(solution)/shard_map/ppermute | solution.py:340
  76.3 6.5 %collective-permute-start.32 = (f32[96,384]{1,0:T(8,128)S(1)}, f32[96,384]{1,0:T(8,128)S(1)}, u32[]{:S(2)}, u32[]{:S(2)}) collective-permute-start(f32[96,384]{1,0:T(8,128)S(1)} %collective-permute-done.24.refs_6_), channel_id=1, source_target_pairs={{0,2},{1,9},{2,0},{3,11},{4,6},{5,13},{6,4},{7,15},{8,10},{9,1},{1... | collective-permute-start | bytes 442376 | tf_op jit(solution)/shard_map/ppermute | solution.py:340
  99.3 6.8 %collective-permute-start.42 = (f32[584,128]{1,0:T(8,128)S(1)}, f32[584,128]{1,0:T(8,128)S(1)}, u32[]{:S(2)}, u32[]{:S(2)}) collective-permute-start(f32[584,128]{1,0:T(8,128)S(1)} %get-tuple-element.108), channel_id=1, source_target_pairs={{0,2},{1,9},{2,0},{3,11},{4,6},{5,13},{6,4},{7,15},{8,10},{9,1},{1... | collective-permute-start | bytes 897032 | tf_op jit(solution)/shard_map/ppermute | solution.py:340
  100.1 10.3 %collective-permute-start.37 = (f32[576,128]{1,0:T(8,128)S(1)}, f32[576,128]{1,0:T(8,128)S(1)}, u32[]{:S(2)}, u32[]{:S(2)}) collective-permute-start(f32[576,128]{1,0:T(8,128)S(1)} %get-tuple-element.99), channel_id=1, source_target_pairs={{0,2},{1,9},{2,0},{3,11},{4,6},{5,13},{6,4},{7,15},{8,10},{9,1},{1... | collective-permute-start | bytes 884744 | tf_op jit(solution)/shard_map/ppermute | solution.py:340
  110.5 6.4 %collective-permute-start.38 = (f32[288,128]{1,0:T(8,128)S(1)}, f32[288,128]{1,0:T(8,128)S(1)}, u32[]{:S(2)}, u32[]{:S(2)}) collective-permute-start(f32[288,128]{1,0:T(8,128)S(1)} %get-tuple-element.101), channel_id=1, source_target_pairs={{0,4},{1,3},{2,6},{3,1},{4,0},{5,7},{6,2},{7,5},{8,12},{9,11},{10,... | collective-permute-start | bytes 442376 | tf_op jit(solution)/shard_map/ppermute | solution.py:340
  117.0 11.2 %collective-permute-start.45 = (f32[152,128]{1,0:T(8,128)S(1)}, f32[152,128]{1,0:T(8,128)S(1)}, u32[]{:S(2)}, u32[]{:S(2)}) collective-permute-start(f32[152,128]{1,0:T(8,128)S(1)} %shard_map.110.refs_2_), channel_id=1, source_target_pairs={{0,16},{1,17},{2,18},{3,19},{4,20},{5,21},{6,22},{7,23},{8,24},{9,... | collective-permute-start | bytes 233480 | tf_op jit(solution)/shard_map/ppermute | solution.py:340
  122.0 6.2 %collective-permute-start.40 = (f32[144,128]{1,0:T(8,128)S(1)}, f32[144,128]{1,0:T(8,128)S(1)}, u32[]{:S(2)}, u32[]{:S(2)}) collective-permute-start(f32[144,128]{1,0:T(8,128)S(1)} %shard_map.105.refs_0_), channel_id=1, source_target_pairs={{0,16},{1,17},{2,18},{3,19},{4,20},{5,21},{6,22},{7,23},{8,24},{9,... | collective-permute-start | bytes 221192 | tf_op jit(solution)/shard_map/ppermute | solution.py:340
  128.3 6.4 %collective-permute-start.46 = (f32[96,384]{1,0:T(8,128)S(1)}, f32[96,384]{1,0:T(8,128)S(1)}, u32[]{:S(2)}, u32[]{:S(2)}) collective-permute-start(f32[96,384]{1,0:T(8,128)S(1)} %get-tuple-element.113.refs_0_), channel_id=1, source_target_pairs={{0,8},{1,9},{2,10},{3,11},{4,12},{5,13},{6,14},{7,15},{8,0},{9,1},... | collective-permute-start | bytes 442376 | tf_op jit(solution)/shard_map/ppermute | solution.py:340
  128.5 6.7 %collective-permute-start.47 = (f32[96,384]{1,0:T(8,128)S(1)}, f32[96,384]{1,0:T(8,128)S(1)}, u32[]{:S(2)}, u32[]{:S(2)}) collective-permute-start(f32[96,384]{1,0:T(8,128)S(1)} %get-tuple-element.113.refs_0_), channel_id=1, source_target_pairs={{0,4},{1,5},{2,6},{3,7},{4,0},{5,1},{6,2},{7,3},{8,12},{9,13},{10,... | collective-permute-start | bytes 442376 | tf_op jit(solution)/shard_map/ppermute | solution.py:340
  129.1 6.2 %collective-permute-start.48 = (f32[96,384]{1,0:T(8,128)S(1)}, f32[96,384]{1,0:T(8,128)S(1)}, u32[]{:S(2)}, u32[]{:S(2)}) collective-permute-start(f32[96,384]{1,0:T(8,128)S(1)} %get-tuple-element.113.refs_0_), channel_id=1, source_target_pairs={{0,12},{1,13},{2,14},{3,15},{4,8},{5,9},{6,10},{7,11},{8,4},{9,5},... | collective-permute-start | bytes 442376 | tf_op jit(solution)/shard_map/ppermute | solution.py:340
  (31 other events, 134.8 us)
